TPU v7x, 128 devices: a whole 4x4x4 slice. The times are simulated.
128 devices in a mesh: dp: 8 (over x, y_hi), tensor: 16 (over z, y_lo, core).
Axes of the slice: x: 4, y: 4 (y_hi: 2, y_lo: 2; y = y_hi * 2 + y_lo), z: 4, core: 2. Of those that a mesh axis runs over, the one named last changes fastest.
Arguments:
- tokens: bfloat16 [16, 256, 8192], P('dp'), may hold values from -6 to 6
- segments: int32 [16, 256], P('dp'), may hold values from 0 to 3, never falling along the last dimension, each value on 1 to 128 neighbouring positions
- norm_gain: float32 [8192], replicated, may hold values from 0.25 to 3.5
- q_weight: bfloat16 [8192, 4096], P('dp', 'tensor'), may hold values from -1.3479223 to 1.3479223
- kv_weight: bfloat16 [2, 8192, 512], P(None, 'dp'), may hold values from -0.055242717 to 0.055242717
- o_weight: bfloat16 [4096, 8192], P('tensor', 'dp'), may hold values from -0.09375 to 0.09375
- basis_query: bfloat16 [8, 8192, 4096], P(None, 'dp', 'tensor'), may hold values from -11 to 11
- basis_output: bfloat16 [8, 4096, 8192], P(None, 'tensor', 'dp'), may hold values from -11 to 11
Outputs:
- next_query: bfloat16 [8192, 4096], P('dp', 'tensor')
- next_output: bfloat16 [4096, 8192], P('tensor', 'dp')
- coefficients: float32 [9], replicated
Inputs may be any that keep to these rules, and one draw needn't show every extreme that they name: `segments`: segment numbers never fall along a sequence.
All inputs are finite; a program needn't handle non-finite values.
Results may differ from a plain program's by a relative error of at most 0.018.
Values may be sent and summed in bfloat16 or wider, within the bound.
A program may use at most 192 MiB of HBM per device.

v0:
```python
import math

import jax
import jax.numpy as jnp
from jax import lax
from jax.sharding import Mesh
from jax.sharding import PartitionSpec as P

D = 8192
HD = 128
QH = 32
KVH = 4
K = 8
DP = ("dp_0", "dp_1")
TENSOR = ("tensor_0", "tensor_1", "tensor_2")
DP_TENSOR = ("dp_0", "dp_1", "tensor_0", "tensor_1", "tensor_2")


PRECISE = lax.Precision.HIGHEST
ROPE_BASE = 500000.0
NORM_EPS = 1e-05
BETA_EPS = 1e-06


def sent_together(arrays, axis, dim, along):
    ends, at = ([], 0)
    for a in arrays[:-1]:
        at += a.shape[along]
        ends.append(at)
    both = jnp.concatenate(arrays, axis=along)
    return tuple(jnp.split(lax.all_gather(both, axis, axis=dim, tiled=True), ends, axis=along))


def filled_up(lines, count):
    spare = -len(lines) % count
    return jnp.pad(lines, [(0, spare)] + [(0, 0)] * (lines.ndim - 1))


def total_of(value, axis):
    lines = value.reshape(-1, *value.shape[1:][-1:])
    own = lax.psum_scatter(
        filled_up(lines, lax.axis_size(axis)), axis, scatter_dimension=0, tiled=True
    )
    whole = lax.all_gather(own, axis).reshape(-1, *lines.shape[1:])
    return lax.slice_in_dim(whole, 0, len(lines)).reshape(value.shape)


def one_axis_at_a_time(value, axes):
    for axis in axes:
        value = lax.psum(value, axis)
    return value


def rope_tables(length, head_width):
    half_width = head_width // 2
    frequency = jnp.exp(
        jnp.arange(half_width, dtype=jnp.float32) * (-2.0 * math.log(ROPE_BASE) / head_width)
    )
    angles = jnp.arange(length, dtype=jnp.float32)[:, None] * frequency[None, :]
    return (jnp.cos(angles), jnp.sin(angles))


def rotate(vectors, cosine_table, sine_table):
    half_width = vectors.shape[-1] // 2
    front_half = vectors[..., :half_width]
    back_half = vectors[..., half_width:]
    return jnp.concatenate(
        [
            front_half * cosine_table - back_half * sine_table,
            front_half * sine_table + back_half * cosine_table,
        ],
        axis=-1,
    )


def attend(query, key_states, values, allowed):
    length = query.shape[1]
    head_width = query.shape[-1]
    cosine_table, sine_table = rope_tables(length, head_width)
    query = rotate(query, cosine_table[:, None, :], sine_table[:, None, :])
    key_states = rotate(key_states, cosine_table, sine_table)
    scores = jnp.einsum("slgd,smd->sglm", query, key_states, precision=PRECISE) * head_width ** (
        -0.5
    )
    scores = jnp.where(allowed[:, None, :, :], scores, -1e30)
    row_max = lax.stop_gradient(jnp.max(scores, axis=-1, keepdims=True))
    weights = jnp.exp(scores - row_max)
    probabilities = weights / jnp.sum(weights, axis=-1, keepdims=True)
    return jnp.einsum("sglm,smd->slgd", probabilities, values, precision=PRECISE)


def allowed_pairs(segments):
    length = segments.shape[1]
    position = jnp.arange(length, dtype=jnp.int32)
    causal = position[:, None] >= position[None, :]
    return jnp.logical_and(segments[:, :, None] == segments[:, None, :], causal[None])


def rms_normed(tokens, norm_gain):
    flat_rows = tokens.reshape(-1, tokens.shape[-1]).astype(jnp.float32)
    inv_rms = lax.rsqrt(jnp.mean(flat_rows * flat_rows, axis=1, keepdims=True) + NORM_EPS)
    return (flat_rows * inv_rms * norm_gain[None, :]).astype(jnp.bfloat16)


def block_products(left_rows, right_rows, block_count, factor):
    left_blocks = left_rows.reshape(block_count, -1, left_rows.shape[1])
    right_blocks = right_rows.reshape(block_count, -1, right_rows.shape[1])
    terms = (
        jnp.einsum("nta,ntb->nab", left_blocks, right_blocks, preferred_element_type=jnp.float32)
        * factor
    )
    rounded = lax.optimization_barrier(terms.astype(jnp.bfloat16))
    return jnp.sum(rounded.astype(jnp.float32), axis=0)


def body(tokens, segments, norm_gain, q_weight, kv_weight, o_weight, basis_query, basis_output):
    groups = lax.axis_size(DP)
    seq_count, length, model_width = tokens.shape
    row_count = seq_count * length
    col_count = q_weight.shape[1]
    heads_dev = col_count // HD
    group_size = QH // KVH
    qwidth = QH * HD
    query_scale = D ** (-0.5)
    output_scale = qwidth ** (-0.5)
    gn_scale = qwidth / (row_count * groups)
    param_count = 2.0 * D * qwidth
    normed = rms_normed(tokens, norm_gain)
    dir_query = basis_query[K - 1]
    dir_output = basis_output[K - 1]
    kv_head = lax.axis_index(TENSOR) * heads_dev // group_size
    kv_columns = lax.dynamic_slice_in_dim(kv_weight, kv_head * HD, HD, 2)
    kv_pair = jnp.concatenate([kv_columns[0], kv_columns[1]], axis=1)
    pieces = sent_together((q_weight, dir_query, kv_pair), DP, 0, 1)
    sum_query = jnp.dot(normed, pieces[0], preferred_element_type=jnp.float32)
    sum_tangent = jnp.dot(normed, pieces[1], preferred_element_type=jnp.float32)
    sum_pair = jnp.dot(normed, pieces[2], preferred_element_type=jnp.float32)
    query = sum_query.astype(jnp.bfloat16)
    tangent = (sum_tangent * query_scale).astype(jnp.bfloat16)
    key_states = sum_pair[:, :HD].astype(jnp.bfloat16)
    values = sum_pair[:, HD:].astype(jnp.bfloat16)
    allowed = allowed_pairs(segments)
    query_wide = query.astype(jnp.float32).reshape(seq_count, length, heads_dev, HD)
    tangent_wide = tangent.astype(jnp.float32).reshape(seq_count, length, heads_dev, HD)
    key_wide = key_states.astype(jnp.float32).reshape(seq_count, length, HD)
    value_wide = values.astype(jnp.float32).reshape(seq_count, length, HD)

    def attend_here(moving):
        return attend(moving, key_wide, value_wide, allowed)

    heads_out, tangent_heads = jax.jvp(attend_here, (query_wide,), (tangent_wide,))
    heads_out = heads_out.reshape(row_count, col_count).astype(jnp.bfloat16)
    tangent_heads = tangent_heads.reshape(row_count, col_count).astype(jnp.bfloat16)
    all_heads, all_tangent = sent_together((heads_out, tangent_heads), DP, 0, 1)
    group_term = jnp.dot(
        all_heads, dir_output, preferred_element_type=jnp.float32
    ) * output_scale + jnp.dot(all_tangent, o_weight, preferred_element_type=jnp.float32)
    tangent_columns = (
        total_of(group_term.astype(jnp.bfloat16), TENSOR).astype(jnp.float32).astype(jnp.bfloat16)
    )
    cot_heads = lax.psum_scatter(
        lax.dot_general(
            tangent_columns, o_weight, (((1,), (1,)), ((), ())), preferred_element_type=jnp.float32
        ).astype(jnp.bfloat16),
        DP,
        scatter_dimension=0,
        tiled=True,
    ).astype(jnp.float32)
    gn_output = block_products(all_heads, tangent_columns, groups, gn_scale * output_scale)
    _, pullback = jax.vjp(attend_here, query_wide)
    cot_query = pullback(cot_heads.reshape(seq_count, length, heads_dev, HD))[0]
    cot_query = cot_query.reshape(row_count, col_count).astype(jnp.bfloat16)
    gn_query = lax.psum_scatter(
        (
            lax.dot_general(
                normed, cot_query, (((0,), (0,)), ((), ())), preferred_element_type=jnp.float32
            )
            * (gn_scale * query_scale)
        ).astype(jnp.bfloat16),
        DP,
        scatter_dimension=0,
        tiled=True,
    ).astype(jnp.float32)

    def local_products(vec_query, vec_output):
        return jnp.sum(basis_query.astype(jnp.float32) * vec_query[None], axis=(1, 2)) + jnp.sum(
            basis_output.astype(jnp.float32) * vec_output[None], axis=(1, 2)
        )

    def remove(vec_query, vec_output, weights_now):
        return (
            vec_query
            - jnp.sum(weights_now[:, None, None] * basis_query.astype(jnp.float32), axis=0),
            vec_output
            - jnp.sum(weights_now[:, None, None] * basis_output.astype(jnp.float32), axis=0),
        )

    local_gram = jnp.einsum(
        "kab,lab->kl", basis_query, basis_query, preferred_element_type=jnp.float32
    ) + jnp.einsum("kab,lab->kl", basis_output, basis_output, preferred_element_type=jnp.float32)
    first_sum, gram_sum = (
        one_axis_at_a_time(local_products(gn_query, gn_output), DP_TENSOR),
        one_axis_at_a_time(local_gram, DP_TENSOR),
    )
    first_coeffs = first_sum / param_count
    gram_matrix = gram_sum / param_count
    kept_query, kept_output = remove(gn_query, gn_output, first_coeffs)
    kept_squares = jnp.sum(kept_query * kept_query) + jnp.sum(kept_output * kept_output)
    second_sum, kept_sum = (
        one_axis_at_a_time(local_products(kept_query, kept_output), DP_TENSOR),
        one_axis_at_a_time(kept_squares, DP_TENSOR),
    )
    second_coeffs = second_sum / param_count
    clean_query, clean_output = remove(kept_query, kept_output, second_coeffs)
    squares = (
        kept_sum / param_count
        - 2.0 * jnp.sum(second_coeffs * second_coeffs)
        + jnp.sum(second_coeffs[:, None] * gram_matrix * second_coeffs[None, :])
    )
    beta = jnp.sqrt(squares + BETA_EPS)
    coefficients = jnp.concatenate([first_coeffs + second_coeffs, beta[None]])
    return (
        (clean_query / beta).astype(jnp.bfloat16),
        (clean_output / beta).astype(jnp.bfloat16),
        coefficients,
    )


def solution(mesh):
    finer = Mesh(
        mesh.devices.reshape(4, 2, 4, 2, 2), ("dp_0", "dp_1", "tensor_0", "tensor_1", "tensor_2")
    )
    placed = (
        P(DP, None, None),
        P(DP, None),
        P(),
        P(DP, TENSOR),
        P(None, DP, None),
        P(TENSOR, DP),
        P(None, DP, TENSOR),
        P(None, TENSOR, DP),
    )
    return jax.shard_map(
        body,
        mesh=finer,
        in_specs=placed,
        out_specs=(P(DP, TENSOR), P(TENSOR, DP), P()),
        check_vma=False,
    )
```

profile of v0, /device:TPU:1, one launch (start us, length us, event | category | flops | bytes accessed | tf_op | source)
XLA Modules:
  0.0 737.6 jit_solution(7066520657061937859)
XLA Ops:
  7.3 1.1 slice_bitcast_fusion
  8.4 1.1 dynamic-slice_bitcast_fusion.1
  9.4 2.4 pad_maximum_fusion
  11.9 5.1 multiply_reduce_fusion
  17.1 0.5 fusion.91
  17.6 0.9 compare_and_fusion.1
  18.5 10.5 %fusion.1 = bf16[512,8192]{1,0:T(8,128)(2,1)} fusion(f32[8192]{0:T(1024)S(1)} %copy-done.11, f32[512]{0:T(512)S(1)} %bitcast.141, bf16[2,256,8192]{2,1,0:T(8,128)(2,1)} %param.8), kind=kLoop, calls=%fused_computation.2 | loop fusion | flops 16777216 | bytes 16812032 | tf_op jit(solution)/shard_map/convert_element_type | solution.py:102
  29.0 133.2 %all-gather.5.cloned.1.call-done = bf16[8192,768]{1,0:T(8,128)(2,1)} async-done(((bf16[1024,768]{1,0:T(8,128)(2,1)}), bf16[8192,768]{1,0:T(8,128)(2,1)}) %all-gather.5.cloned.1.call-update) | async-done | bytes 12582928 | tf_op jit(solution)/shard_map/all_gather | solution.py:31
  162.2 6.9 fusion.31
  169.3 7.1 fusion.40
  176.7 7.0 fusion.25
  183.7 0.4 fusion.105
  184.1 1.1 fusion.103
  185.7 1.2 fusion.65
  187.1 1.4 fusion.43
  188.6 1.8 copy.31
  190.4 1.7 copy.95
  192.1 1.4 fusion.106
  193.5 1.7 fusion.44
  195.5 1.8 pad_maximum_fusion.1
  197.3 69.5 %all-gather.7.cloned.1.call-done = bf16[4096,512]{1,0:T(8,128)(2,1)} async-done(((bf16[512,512]{1,0:T(8,128)(2,1)}), bf16[4096,512]{1,0:T(8,128)(2,1)}) %all-gather.7.cloned.1.call-update) | async-done | bytes 4194320 | tf_op jit(solution)/shard_map/all_gather | solution.py:31
  266.9 9.9 %fusion.72 = f32[4096,1024]{1,0:T(8,128)} fusion(bf16[8,256,1024]{2,1,0:T(8,128)(2,1)} %param.15, bf16[4096,512]{1,0:T(8,128)(2,1)} %all-gather.7.cloned.1.call-done), kind=kOutput, calls=%fused_computation.83 | convolution fusion | flops 2147483648 | bytes 19398656 | tf_op jit(solution)/shard_map/dot_general | solution.py:155
  276.8 9.3 %add_convert_fusion = bf16[4096,1024]{1,0:T(8,128)(2,1)} fusion(f32[4096,1024]{1,0:T(8,128)} %fusion.72, bf16[256,1024]{1,0:T(8,128)(2,1)S(1)} %copy-done, bf16[4096,512]{1,0:T(8,128)(2,1)S(1)} %copy-done.5), kind=kOutput, calls=%fused_computation.3 | convolution fusion | flops 2160066560 | bytes 27787264 | tf_op jit(solution)/shard_map/dot_general | solution.py:157
  286.1 94.6 %reduce-scatter.4.cloned.1.call-done = bf16[256,1024]{1,0:T(8,128)(2,1)} async-done(((bf16[4096,1024]{1,0:T(8,128)(2,1)}), bf16[256,1024]{1,0:T(8,128)(2,1)}) %reduce-scatter.4.cloned.1.call-update) | async-done | bytes 524304 | tf_op jit(solution)/shard_map/reduce_scatter | solution.py:41
  380.8 54.6 %all-gather.9.cloned.1.call-done = bf16[4096,1024]{1,0:T(8,128)(2,1)} async-done(((bf16[256,1024]{1,0:T(8,128)(2,1)}), bf16[4096,1024]{1,0:T(8,128)(2,1)}) %all-gather.9.cloned.1.call-update) | async-done | bytes 8388624 | tf_op jit(solution)/shard_map/all_gather | solution.py:44
  435.3 7.1 convolution_convert_fusion
  443.0 9.9 %multiply_convert_fusion = bf16[2,256,8192]{2,1,0:T(8,128)(2,1)} fusion(f32[8192]{0:T(1024)S(1)} %copy-done.12, f32[2,256]{1,0:T(2,128)S(1)} %get-tuple-element.43, bf16[2,256,8192]{2,1,0:T(8,128)(2,1)} %param.8), kind=kLoop, calls=%fused_computation.4 | loop fusion | flops 16777216 | bytes 16812032 | tf_op jit(solution)/shard_map/convert_element_type | solution.py:102
  452.9 64.1 %reduce-scatter.6.cloned.1.call-done = bf16[512,256]{1,0:T(8,128)(2,1)} async-done(((bf16[4096,256]{1,0:T(8,128)(2,1)}), bf16[512,256]{1,0:T(8,128)(2,1)}) %reduce-scatter.6.cloned.1.call-update) | async-done | bytes 262160 | tf_op jit(solution)/shard_map/reduce_scatter | solution.py:161
  517.0 1.0 reshape.215
  518.2 0.4 multiply_reduce_fusion.3
  518.6 2.1 fusion.63
  521.5 4.4 fusion.2
  526.0 1.6 slice-done
  527.5 5.9 multiply_convert_fusion.1
  533.5 1.1 convert_reduce_fusion
  534.5 1.1 fusion.7
  535.7 74.3 %reduce-scatter.8.cloned.1.call-done = bf16[1024,256]{1,0:T(8,128)(2,1)} async-done(((bf16[8192,256]{1,0:T(8,128)(2,1)}), bf16[1024,256]{1,0:T(8,128)(2,1)}) %reduce-scatter.8.cloned.1.call-update) | async-done | bytes 524304 | tf_op jit(solution)/shard_map/reduce_scatter | solution.py:173
  610.0 1.1 convert_element_type.112
  611.1 3.4 fusion.3
  614.5 7.6 %psum.140 = f32[8]{0:T(128)S(1)} all-reduce(f32[8]{0:T(128)S(1)} %add.117), channel_id=1, replica_groups=mesh['dp_0'=4,'dp_1'=2,'tensor_0'=4,'tensor_1'=2,'tensor_2'=2] {'dp_0'}, use_global_device_ids=true, to_apply=%region_11.12 | all-reduce | flops 8 | bytes 64 | tf_op jit(solution)/shard_map/psum | solution.py:50
  622.2 5.3 psum.141
  627.4 8.8 %psum.142 = f32[8]{0:T(128)S(1)} all-reduce(f32[8]{0:T(128)S(1)} %psum.141), channel_id=1, replica_groups=mesh['dp_0'=4,'dp_1'=2,'tensor_0'=4,'tensor_1'=2,'tensor_2'=2] {'tensor_0'}, use_global_device_ids=true, to_apply=%region_13.14 | all-reduce | flops 8 | bytes 64 | tf_op jit(solution)/shard_map/psum | solution.py:50
  636.2 9.0 %fusion.45 = f32[8,8]{1,0:T(8,128)S(1)} fusion(bf16[8,1024,256]{2,1,0:T(8,128)(2,1)} %param.14), kind=kOutput, calls=%fused_computation.54 | convolution fusion | flops 33554432 | bytes 4194560 | tf_op jit(solution)/shard_map/kab,lab->kl/dot_general | solution.py:198
  645.2 4.0 psum.143
  649.2 8.4 %fusion.51 = f32[8,8]{1,0:T(8,128)S(1)} fusion(f32[8,8]{1,0:T(8,128)S(1)} %fusion.45, bf16[8,256,1024]{2,1,0:T(8,128)(2,1)} %param.15), kind=kOutput, calls=%fused_computation.56 | convolution fusion | flops 33554496 | bytes 4194816 | tf_op jit(solution)/shard_map/kab,lab->kl/dot_general | solution.py:200
  657.7 10.6 %psum.144 = f32[8]{0:T(128)S(1)} all-reduce(f32[8]{0:T(128)S(1)} %psum.143), channel_id=1, replica_groups=mesh['dp_0'=4,'dp_1'=2,'tensor_0'=4,'tensor_1'=2,'tensor_2'=2] {'tensor_2'}, use_global_device_ids=true, to_apply=%region_15.16 | all-reduce | flops 8 | bytes 64 | tf_op jit(solution)/shard_map/psum | solution.py:50
  668.3 3.6 fusion.8
  671.9 3.4 fusion.4
  675.2 0.9 multiply_reduce_fusion.1
  676.2 1.3 fusion.9
  677.5 0.9 multiply_reduce_fusion.2
  678.4 1.2 fusion.5
  680.9 6.6 all-reduce.3
  687.5 6.0 all-reduce.6
  693.5 6.7 all-reduce.2
  700.2 4.5 all-reduce.5
  704.7 8.8 %all-reduce.4 = (f32[8]{0:T(128)S(1)}, f32[]{:T(128)}, f32[8,8]{1,0:T(8,128)S(1)}) all-reduce(f32[8]{0:T(128)S(1)} %get-tuple-element.12, f32[]{:T(128)} %get-tuple-element.13, f32[8,8]{1,0:T(8,128)S(1)} %get-tuple-element.14), channel_id=1, replica_groups=mesh['dp_0'=4,'dp_1'=2,'tensor_0'=4,'tensor_1'=2,'tensor_2'=2] {'tensor_2'}, use_global_device_ids=true, to_apply=%region_24.25 | all-reduce | flops 73 | bytes 584 | tf_op jit(solution)/shard_map/psum | solution.py:50
  713.5 0.6 fusion.100
  714.1 4.4 fusion.10
  718.5 4.2 fusion.6
  722.7 0.7 multiply_reduce_fusion.4
  725.3 2.2 divide_convert_fusion
  727.5 2.2 divide_convert_fusion.1
  729.7 0.6 pad_maximum_fusion.2
  (64 shorter events, 3.3 us)
Async XLA Ops:
  7.2 269.6 %copy-start = (bf16[256,1024]{1,0:T(8,128)(2,1)S(1)}, bf16[256,1024]{1,0:T(8,128)(2,1)}, u32[]{:S(2)}) copy-start(bf16[256,1024]{1,0:T(8,128)(2,1)} %param.13) | copy-start | bytes 1572868
  7.2 10.4 %copy-start.13 = (s32[2,256]{1,0:T(2,128)S(1)}, s32[2,256]{1,0:T(2,128)}, u32[]{:S(2)}) copy-start(s32[2,256]{1,0:T(2,128)} %param.9) | copy-start | bytes 6148
  7.2 11.3 %copy-start.11 = (f32[8192]{0:T(1024)S(1)}, f32[8192]{0:T(1024)}, u32[]{:S(2)}) copy-start(f32[8192]{0:T(1024)} %param.10) | copy-start | bytes 98308
  7.2 155.0 %all-gather.5.cloned.1.call-start = ((), (), s32[]{:S(2)}) async-start(), calls=%async_computation.3 | async-start | bytes 14155776 | tf_op jit(solution)/shard_map/all_gather | solution.py:31
  11.8 255.0 %all-gather.7.cloned.1.call-start = ((), (), s32[]{:S(2)}) async-start(), calls=%async_computation.4 | async-start | bytes 4718592 | tf_op jit(solution)/shard_map/all_gather | solution.py:31
  184.0 3.1 copy-start.9
  197.3 183.4 %reduce-scatter.4.cloned.1.call-start = ((), (), s32[]{:S(2)}) async-start(), calls=%async_computation.5 | async-start | bytes 8912896 | tf_op jit(solution)/shard_map/reduce_scatter | solution.py:41
  266.9 9.9 %copy-start.5 = (bf16[4096,512]{1,0:T(8,128)(2,1)S(1)}, bf16[4096,512]{1,0:T(8,128)(2,1)}, u32[]{:S(2)}) copy-start(bf16[4096,512]{1,0:T(8,128)(2,1)} %all-gather.7.cloned.1.call-done) | copy-start | bytes 12582916
  286.1 149.3 %all-gather.9.cloned.1.call-start = ((), (), s32[]{:S(2)}) async-start(), calls=%async_computation.8 | async-start | bytes 8912896 | tf_op jit(solution)/shard_map/all_gather | solution.py:44
  380.7 62.0 %copy-start.8 = (pred[2,256,256]{1,2,0:T(8,128)(4,1)S(1)}, pred[2,256,256]{1,2,0:T(8,128)(4,1)}, u32[]{:S(2)}) copy-start(pred[2,256,256]{1,2,0:T(8,128)(4,1)} %get-tuple-element.40) | copy-start | bytes 393220
  380.7 62.3 %copy-start.12 = (f32[8192]{0:T(1024)S(1)}, f32[8192]{0:T(1024)}, u32[]{:S(2)}) copy-start(f32[8192]{0:T(1024)} %param.10) | copy-start | bytes 98308
  380.7 136.2 %reduce-scatter.6.cloned.1.call-start = ((), (), s32[]{:S(2)}) async-start(), calls=%async_computation.6 | async-start | bytes 2359296 | tf_op jit(solution)/shard_map/reduce_scatter | solution.py:161
  442.5 167.5 %reduce-scatter.8.cloned.1.call-start = ((), (), s32[]{:S(2)}) async-start(), calls=%async_computation.7 | async-start | bytes 4718592 | tf_op jit(solution)/shard_map/reduce_scatter | solution.py:173
  443.0 75.2 %copy-start.10 = (bf16[512,128]{1,0:T(8,128)(2,1)S(1)}, bf16[512,128]{1,0:T(8,128)(2,1)}, u32[]{:S(2)}) copy-start(bf16[512,128]{1,0:T(8,128)(2,1)} %copy-done.9) | copy-start | bytes 393220
  518.2 3.4 copy-start.6
  525.9 1.6 slice-start
  527.5 7.0 copy-start.2
  668.3 7.9 %copy-start.3 = (bf16[8,256,1024]{2,1,0:T(8,128)(2,1)S(1)}, bf16[8,256,1024]{2,1,0:T(8,128)(2,1)}, u32[]{:S(2)}) copy-start(bf16[8,256,1024]{2,1,0:T(8,128)(2,1)} %param.15) | copy-start | bytes 12582916
  668.3 9.2 %copy-start.7 = (bf16[1024,256]{1,0:T(8,128)(2,1)S(1)}, bf16[1024,256]{1,0:T(8,128)(2,1)}, u32[]{:S(2)}) copy-start(bf16[1024,256]{1,0:T(8,128)(2,1)} %reduce-scatter.8.cloned.1.call-done) | copy-start | bytes 1572868
  671.9 6.5 copy-start.4
  678.4 51.9 %copy-start.1 = (bf16[256,1024]{1,0:T(8,128)(2,1)S(1)}, bf16[256,1024]{1,0:T(8,128)(2,1)}, u32[]{:S(2)}) copy-start(bf16[256,1024]{1,0:T(8,128)(2,1)} %param.13) | copy-start | bytes 1572868
Sparse Core Ops, SparseCore 0:
  11.9 150.1 all-gather.4
  197.4 69.4 all-gather.6
  286.2 94.4 reduce-scatter.3
  382.2 53.0 all-gather.8
  442.6 74.3 reduce-scatter.5
  526.1 83.8 reduce-scatter.7
where the time goes:
time: 747 us; the launch traced here: 738 us
  waiting for transfers between devices  490 us (66%)
  matrix products  83.3 us (11%)
  blocking collectives  69 us (9%)
  other arithmetic  65 us (9%)
  between operations  18.3 us (2%)
  local copies, waits for them, and re-layouts  11.3 us (2%)
    all_gather x2, waiting for transfers between devices, sent_together(): lax.all_gather(both, axis, axis=dim, tiled=True)  203 us
    reduce_scatter x1, waiting for transfers between devices, total_of(): lax.psum_scatter(filled_up(lines, lax.axis_size(axis)), axis, scatter_dim...  94.6 us
    reduce_scatter x1, waiting for transfers between devices, body(): lax.psum_scatter((lax.dot_general(normed, cot_query, (((0,), (0,)), ((),...  74.3 us
    psum x10, blocking collectives, one_axis_at_a_time(): value = lax.psum(value, axis)  69 us
    reduce_scatter x1, waiting for transfers between devices, body(): lax.psum_scatter(lax.dot_general(tangent_columns, o_weight, (((1,), (1,))...  64.1 us
    all_gather x1, waiting for transfers between devices, total_of(): whole = lax.all_gather(own, axis).reshape(-1, *lines.shape[1:])  54.6 us
    convert_element_type x2, other arithmetic, rms_normed(): return (flat_rows * inv_rms * norm_gain[None, :]).astype(jnp.bfloat16)  20.4 us
  transfers between devices with their start and end apart: 6, of which 6 were waited for; matrix products, arithmetic and copies ran while one was open for 5% of the time, Pallas kernels for 0%

commit v1 on v0

--- a/solution.py
+++ b/solution.py
@@ -1,8 +1,11 @@
+import functools
 import math
 
 import jax
 import jax.numpy as jnp
 from jax import lax
+from jax.experimental import pallas as pl
+from jax.experimental.pallas import tpu as pltpu
 from jax.sharding import Mesh
 from jax.sharding import PartitionSpec as P
 
@@ -22,6 +25,64 @@
 BETA_EPS = 1e-06
 
 
+MESH = pl.DeviceIdType.MESH
+VMEM_BYTES = 58 * 1024 * 1024
+X1, X3, X2, YH = (1, 0, 0, 0, 0), (3, 0, 0, 0, 0), (2, 0, 0, 0, 0), (0, 1, 0, 0, 0)
+Z1, Z3, YL, CORE = (0, 0, 1, 0, 0), (0, 0, 3, 0, 0), (0, 0, 0, 1, 0), (0, 0, 0, 0, 1)
+BF = jnp.bfloat16
+F32 = jnp.float32
+
+
+def position():
+    return [lax.axis_index(a) for a in DP_TENSOR]
+
+
+def flipped(value, mask):
+    if mask == 0:
+        return value
+    if mask == 1:
+        return value + 1 - 2 * lax.rem(value, 2)
+    if mask == 2:
+        return lax.rem(value + 2, 4)
+    return 3 - value
+
+
+def peer(here, masks):
+    return tuple(flipped(v, m) for v, m in zip(here, masks))
+
+
+def greet(here, peers):
+    barrier = pltpu.get_barrier_semaphore()
+    for masks in peers:
+        pl.semaphore_signal(barrier, inc=1, device_id=peer(here, masks), device_id_type=MESH)
+    pl.semaphore_wait(barrier, len(peers))
+
+
+def send(src, dst, send_sem, recv_sem, here, masks):
+    copy = pltpu.make_async_remote_copy(
+        src_ref=src,
+        dst_ref=dst,
+        send_sem=send_sem,
+        recv_sem=recv_sem,
+        device_id=peer(here, masks),
+        device_id_type=MESH,
+    )
+    copy.start()
+    return copy
+
+
+def dp_source(here, first, second, third, kind):
+    x, yh = here[0], here[1]
+    low, high = (first, third) if kind == 0 else (third, first)
+    x = x + low * (1 - 2 * lax.rem(x, 2))
+    x = x + high * (3 - 2 * x)
+    yh = yh + second * (1 - 2 * yh)
+    return x * 2 + yh
+
+
+STAGES = ((X1, YH, X3), (X3, YH, X1))
+
+
 def sent_together(arrays, axis, dim, along):
     ends, at = ([], 0)
     for a in arrays[:-1]:
@@ -43,12 +104,6 @@
     )
     whole = lax.all_gather(own, axis).reshape(-1, *lines.shape[1:])
     return lax.slice_in_dim(whole, 0, len(lines)).reshape(value.shape)
-
-
-def one_axis_at_a_time(value, axes):
-    for axis in axes:
-        value = lax.psum(value, axis)
-    return value
 
 
 def rope_tables(length, head_width):
@@ -96,12 +151,6 @@
     return jnp.logical_and(segments[:, :, None] == segments[:, None, :], causal[None])
 
 
-def rms_normed(tokens, norm_gain):
-    flat_rows = tokens.reshape(-1, tokens.shape[-1]).astype(jnp.float32)
-    inv_rms = lax.rsqrt(jnp.mean(flat_rows * flat_rows, axis=1, keepdims=True) + NORM_EPS)
-    return (flat_rows * inv_rms * norm_gain[None, :]).astype(jnp.bfloat16)
-
-
 def block_products(left_rows, right_rows, block_count, factor):
     left_blocks = left_rows.reshape(block_count, -1, left_rows.shape[1])
     right_blocks = right_rows.reshape(block_count, -1, right_rows.shape[1])
@@ -111,6 +160,402 @@
     )
     rounded = lax.optimization_barrier(terms.astype(jnp.bfloat16))
     return jnp.sum(rounded.astype(jnp.float32), axis=0)
+
+
+SUPER = (0, 1, 0, 1, 2, 3, 2, 3)
+HALF = (0, 0, 1, 1, 0, 0, 1, 1)
+
+
+def project_kernel(
+    tok, gain, q_w, vec_q, kv_w, vec_o,
+    q_out, t_out, k_out, v_out, normed_out, gram_out,
+    x, buf, acc, mine, theirs, vq, vo, load, sent, got,
+):
+    here = position()
+    core = here[4]
+    kv_head = here[2]
+    for_rows = []
+    for s in range(4):
+        rows = pl.ds(s * 256, 256)
+        kv_cols = pl.ds(pl.multiple_of(kv_head * HD, HD), HD)
+        parts = (
+            (q_w.at[rows], buf.at[s, 0, :, pl.ds(0, 256)]),
+            (vec_q.at[K - 1, rows], buf.at[s, 0, :, pl.ds(256, 256)]),
+            (kv_w.at[core, rows, kv_cols], buf.at[s, 0, :, pl.ds(512, 128)]),
+        )
+        for n, (src, dst) in enumerate(parts):
+            copy = pltpu.make_async_copy(src, dst, load.at[3 * s + n])
+            copy.start()
+            for_rows.append(copy)
+    tok_copy = pltpu.make_async_copy(tok, x, load.at[12])
+    tok_copy.start()
+    vq_copy = pltpu.make_async_copy(vec_q, vq, load.at[13])
+    vq_copy.start()
+    vo_copy = pltpu.make_async_copy(vec_o, vo, load.at[14])
+    vo_copy.start()
+    greet(here, (X1, X3, YH, CORE))
+    for copy in for_rows:
+        copy.wait()
+
+    def start_stage(stage, k):
+        s, rows = SUPER[k], pl.ds(HALF[k] * 128, 128)
+        n = 1 << stage
+        at = stage * 8 + k
+        return send(
+            buf.at[s, pl.ds(0, n), rows],
+            buf.at[s, pl.ds(n, n), rows],
+            sent.at[at],
+            got.at[at],
+            here,
+            STAGES[s % 2][stage],
+        )
+
+    first = [start_stage(0, k) for k in range(8)]
+
+    def norm_rows(lo, hi):
+        def step(i, carry):
+            rows = pl.ds(pl.multiple_of(i * 16, 16), 16)
+            total = jnp.zeros((16, 1), F32)
+            for c in range(8):
+                part = x[rows, pl.ds(c * 1024, 1024)].astype(F32)
+                total += jnp.sum(part * part, axis=1, keepdims=True)
+            inv = lax.rsqrt(total / D + NORM_EPS)
+            for c in range(8):
+                cols = pl.ds(c * 1024, 1024)
+                x[rows, cols] = (x[rows, cols].astype(F32) * inv * gain[:, cols]).astype(BF)
+            return carry
+
+        lax.fori_loop(lo // 16, hi // 16, step, 0)
+
+    def dots(s, lo, hi):
+        def step(p, carry):
+            source = dp_source(here, lax.rem(p, 2), lax.rem(p // 2, 2), p // 4, s % 2)
+            cols = pl.ds(pl.multiple_of(source * 1024 + s * 256, 256), 256)
+            acc[...] += jnp.dot(x[:, cols], buf[s, p], preferred_element_type=F32)
+            return carry
+
+        lax.fori_loop(lo, hi, step, 0)
+
+    def gram():
+        pairs = [(i, j) for i in range(K) for j in range(i, K)]
+
+        def tile(ref, rows, cols, carry):
+            b = [ref[j, rows, cols].astype(F32) for j in range(K)]
+            out = []
+            for (i, j), a in zip(pairs, carry):
+                p = b[i] * b[j]
+                out.append(a + (p[:8] + p[8:]))
+            return tuple(out)
+
+        def step_q(r, carry):
+            rows = pl.ds(pl.multiple_of(r * 16, 16), 16)
+            for h in range(2):
+                carry = tile(vq, rows, pl.ds(h * 128, 128), carry)
+            return carry
+
+        def step_o(r, carry):
+            rows = pl.ds(pl.multiple_of(r * 16, 16), 16)
+            for h in range(8):
+                carry = tile(vo, rows, pl.ds(h * 128, 128), carry)
+            return carry
+
+        carry = tuple(jnp.zeros((8, 128), F32) for _ in pairs)
+        carry = lax.fori_loop(0, 64, step_q, carry)
+        carry = lax.fori_loop(0, 16, step_o, carry)
+        for (i, j), a in zip(pairs, carry):
+            line = jnp.sum(a, axis=0, keepdims=True)
+            gram_out[pl.ds(i * 8 + j, 1)] = line
+            if i != j:
+                gram_out[pl.ds(j * 8 + i, 1)] = line
+
+    acc[...] = jnp.zeros_like(acc)
+    second, third = [], []
+    out_copy = None
+    for k in range(8):
+        first[k].wait_recv()
+        second.append(start_stage(1, k))
+        if k == 0:
+            tok_copy.wait()
+            norm_rows(0, 256)
+        if k >= 1:
+            second[k - 1].wait_recv()
+            third.append(start_stage(2, k - 1))
+        if k == 1:
+            norm_rows(256, 512)
+            out_copy = pltpu.make_async_copy(x, normed_out, load.at[15])
+            out_copy.start()
+        if k == 2:
+            vq_copy.wait()
+            vo_copy.wait()
+            gram()
+        if k == 4:
+            dots(0, 0, 4)
+        if k == 5:
+            dots(1, 0, 4)
+        if k == 7:
+            dots(2, 0, 4)
+    second[7].wait_recv()
+    third.append(start_stage(2, 7))
+    dots(3, 0, 4)
+    for s, (k0, k1) in enumerate(((0, 2), (1, 3), (4, 6), (5, 7))):
+        third[k0].wait_recv()
+        third[k1].wait_recv()
+        dots(s, 4, 8)
+    mine[...] = acc[:, pl.ds(512, 128)].astype(BF)
+    swap = send(mine, theirs, sent.at[24], got.at[24], here, CORE)
+    q_out[...] = acc[:, pl.ds(0, 256)].astype(BF)
+    t_out[...] = (acc[:, pl.ds(256, 256)] * (D ** (-0.5))).astype(BF)
+    swap.wait()
+    own = mine[...].astype(F32)
+    other = theirs[...].astype(F32)
+    first_core = core == 0
+    k_out[...] = jnp.where(first_core, own, other).astype(BF)
+    v_out[...] = jnp.where(first_core, other, own).astype(BF)
+    for copy in first + second + third:
+        copy.wait_send()
+    out_copy.wait()
+
+
+def any_specs(n):
+    return [pl.BlockSpec(memory_space=pl.ANY) for _ in range(n)]
+
+
+def vmem_specs(n):
+    return [pl.BlockSpec(memory_space=pltpu.VMEM) for _ in range(n)]
+
+
+def project(tokens, norm_gain, q_weight, basis_query, kv_weight, basis_output):
+    shape = jax.ShapeDtypeStruct
+    return pl.pallas_call(
+        project_kernel,
+        out_shape=(
+            shape((512, 256), BF),
+            shape((512, 256), BF),
+            shape((512, HD), BF),
+            shape((512, HD), BF),
+            shape((512, D), BF),
+            shape((64, 128), F32),
+        ),
+        in_specs=any_specs(1) + vmem_specs(1) + any_specs(4),
+        out_specs=tuple(vmem_specs(4) + any_specs(1) + vmem_specs(1)),
+        scratch_shapes=[
+            pltpu.VMEM((512, D), BF),
+            pltpu.VMEM((4, 8, 256, 640), BF),
+            pltpu.VMEM((512, 640), F32),
+            pltpu.VMEM((512, HD), BF),
+            pltpu.VMEM((512, HD), BF),
+            pltpu.VMEM((K, 1024, 256), BF),
+            pltpu.VMEM((K, 256, 1024), BF),
+            pltpu.SemaphoreType.DMA((16,)),
+            pltpu.SemaphoreType.DMA((25,)),
+            pltpu.SemaphoreType.DMA((25,)),
+        ],
+        compiler_params=pltpu.CompilerParams(
+            collective_id=0, has_side_effects=True, vmem_limit_bytes=VMEM_BYTES
+        ),
+        name="project",
+    )(tokens, norm_gain, q_weight, basis_query, kv_weight, basis_output)
+
+
+def query_grad_kernel(factor, normed, cot, out, part, r1, r2, r3, sent, got):
+    here = position()
+    greet(here, (X1, X3, YH))
+    copies = []
+
+    def product(low, mid, high):
+        source = dp_source(here, low, mid, high, 0)
+        cols = pl.ds(pl.multiple_of(source * 1024, 1024), 1024)
+        block = jnp.dot(cot[...], normed[:, cols], preferred_element_type=F32) * factor
+        block = block.astype(BF)
+        for c in range(8):
+            place = low + 2 * mid + 4 * high if c % 2 == 0 else high + 2 * mid + 4 * low
+            part[c, place] = block[:, c * 128 : (c + 1) * 128]
+
+    def start(stage, c, src, dst):
+        at = stage * 8 + c
+        copy = send(src, dst, sent.at[at], got.at[at], here, STAGES[c % 2][2 - stage])
+        copies.append(copy)
+        return copy
+
+    def start_first(c):
+        return start(0, c, part.at[c, pl.ds(4, 4)], r1.at[c])
+
+    product(1, 0, 1)
+    product(1, 1, 1)
+    product(0, 0, 1)
+    product(0, 1, 1)
+    one = {c: start_first(c) for c in (0, 2, 4, 6)}
+    product(1, 0, 0)
+    product(1, 1, 0)
+    one.update({c: start_first(c) for c in (1, 3, 5, 7)})
+    product(0, 0, 0)
+    product(0, 1, 0)
+
+    def added(c, n, ref):
+        part[c, pl.ds(0, n)] = (
+            part[c, pl.ds(0, n)].astype(F32) + ref[c].astype(F32)
+        ).astype(BF)
+
+    two, three = {}, {}
+    for c in range(8):
+        one[c].wait_recv()
+        added(c, 4, r1)
+        two[c] = start(1, c, part.at[c, pl.ds(2, 2)], r2.at[c])
+        if c >= 1:
+            two[c - 1].wait_recv()
+            added(c - 1, 2, r2)
+            three[c - 1] = start(2, c - 1, part.at[c - 1, pl.ds(1, 1)], r3.at[c - 1])
+    two[7].wait_recv()
+    added(7, 2, r2)
+    three[7] = start(2, 7, part.at[7, pl.ds(1, 1)], r3.at[7])
+    for c in range(8):
+        three[c].wait_recv()
+        total = part[c, 0].astype(F32) + r3[c, 0].astype(F32)
+        out[pl.ds(c * 128, 128), :] = total.T
+    for copy in copies:
+        copy.wait_send()
+
+
+def query_grad(normed, cot_rows, factor):
+    return pl.pallas_call(
+        functools.partial(query_grad_kernel, factor),
+        out_shape=jax.ShapeDtypeStruct((1024, 256), F32),
+        in_specs=vmem_specs(2),
+        out_specs=pl.BlockSpec(memory_space=pltpu.VMEM),
+        scratch_shapes=[
+            pltpu.VMEM((8, 8, 256, 128), BF),
+            pltpu.VMEM((8, 4, 256, 128), BF),
+            pltpu.VMEM((8, 2, 256, 128), BF),
+            pltpu.VMEM((8, 1, 256, 128), BF),
+            pltpu.SemaphoreType.DMA((24,)),
+            pltpu.SemaphoreType.DMA((24,)),
+        ],
+        compiler_params=pltpu.CompilerParams(
+            collective_id=1, has_side_effects=True, vmem_limit_bytes=VMEM_BYTES
+        ),
+        name="query_grad",
+    )(normed, cot_rows)
+
+
+DP_PEERS = [(x, yh, 0, 0, 0) for x in range(4) for yh in range(2) if x or yh]
+TENSOR_PEERS = [(0, 0, z, yl, c) for z in range(4) for yl in range(2) for c in range(2) if z or yl or c]
+
+
+def sum_over(here, slots_dp, slots_tensor, staged, sent, got, at):
+    dp = here[0] * 2 + here[1]
+    tensor = here[2] * 4 + here[3] * 2 + here[4]
+
+    def exchange(slots, own, peers, base):
+        copies = []
+        for n, masks in enumerate(peers):
+            ref = slots.at[own]
+            copies.append(send(ref, ref, sent.at[base + n], got.at[base + n], here, masks))
+        return copies
+
+    one = exchange(slots_dp, dp, DP_PEERS, at)
+    for copy in one:
+        copy.wait_recv()
+    total = slots_dp[0]
+    for n in range(1, 8):
+        total = total + slots_dp[n]
+    slots_tensor[tensor] = total
+    two = exchange(slots_tensor, tensor, TENSOR_PEERS, at + 7)
+    for copy in two:
+        copy.wait_recv()
+    total = slots_tensor[0]
+    for n in range(1, 16):
+        total = total + slots_tensor[n]
+    for copy in one + two:
+        copy.wait_send()
+    return total
+
+
+def clean_kernel(
+    count, gq, go, vq, vo, gram, next_q, next_o, coeffs,
+    cq, co, s1, s2, u1, u2, sent, got,
+):
+    here = position()
+    dp = here[0] * 2 + here[1]
+    greet(here, DP_PEERS + TENSOR_PEERS)
+
+    def over_tiles(visit, carry):
+        def step_q(r, state):
+            rows = pl.ds(pl.multiple_of(r * 16, 16), 16)
+            for h in range(2):
+                state = visit(gq, vq, cq, rows, pl.ds(h * 128, 128), state)
+            return state
+
+        def step_o(r, state):
+            rows = pl.ds(pl.multiple_of(r * 16, 16), 16)
+            for h in range(8):
+                state = visit(go, vo, co, rows, pl.ds(h * 128, 128), state)
+            return state
+
+        carry = lax.fori_loop(0, 64, step_q, carry)
+        return lax.fori_loop(0, 16, step_o, carry)
+
+    def against_basis(g, v, c, rows, cols, state):
+        here_g = g[rows, cols]
+        out = []
+        for j in range(K):
+            p = here_g * v[j, rows, cols].astype(F32)
+            out.append(state[j] + (p[:8] + p[8:]))
+        return tuple(out)
+
+    zero = jnp.zeros((8, 128), F32)
+    firsts = over_tiles(against_basis, (zero,) * K)
+    s1[dp, pl.ds(0, 64)] = gram[...]
+    for j in range(K):
+        s1[dp, pl.ds(64 + j, 1)] = jnp.sum(firsts[j], axis=0, keepdims=True)
+    total = sum_over(here, s1, s2, None, sent, got, 0)
+    lines = jnp.sum(total, axis=1, keepdims=True) / count
+    first = lines[64:72]
+    second = first
+    for i in range(K):
+        second = second - lines[8 * i : 8 * i + 8] * first[i : i + 1]
+    both = first + second
+    weights = [jnp.broadcast_to(both[j : j + 1], (16, 128)) for j in range(K)]
+
+    def cleaned(g, v, c, rows, cols, state):
+        value = g[rows, cols]
+        for j in range(K):
+            value = value - weights[j] * v[j, rows, cols].astype(F32)
+        c[rows, cols] = value
+        p = value * value
+        return state + (p[:8] + p[8:])
+
+    u1[dp] = over_tiles(cleaned, zero)
+    squares = sum_over(here, u1, u2, None, sent, got, 22)
+    squares = jnp.sum(jnp.sum(squares, axis=1, keepdims=True), axis=0, keepdims=True) / count
+    beta = jnp.sqrt(squares + BETA_EPS)
+    next_q[...] = (cq[...] / beta).astype(BF)
+    next_o[...] = (co[...] / beta).astype(BF)
+    coeffs[pl.ds(0, 8)] = jnp.broadcast_to(both, (8, 128))
+    coeffs[pl.ds(8, 8)] = jnp.broadcast_to(beta, (8, 128))
+
+
+def clean(gn_query, gn_output, basis_query, basis_output, gram, count):
+    shape = jax.ShapeDtypeStruct
+    return pl.pallas_call(
+        functools.partial(clean_kernel, count),
+        out_shape=(shape((1024, 256), BF), shape((256, 1024), BF), shape((16, 128), F32)),
+        in_specs=vmem_specs(5),
+        out_specs=tuple(vmem_specs(3)),
+        scratch_shapes=[
+            pltpu.VMEM((1024, 256), F32),
+            pltpu.VMEM((256, 1024), F32),
+            pltpu.VMEM((8, 72, 128), F32),
+            pltpu.VMEM((16, 72, 128), F32),
+            pltpu.VMEM((8, 8, 128), F32),
+            pltpu.VMEM((16, 8, 128), F32),
+            pltpu.SemaphoreType.DMA((44,)),
+            pltpu.SemaphoreType.DMA((44,)),
+        ],
+        compiler_params=pltpu.CompilerParams(
+            collective_id=2, has_side_effects=True, vmem_limit_bytes=VMEM_BYTES
+        ),
+        name="clean",
+    )(gn_query, gn_output, basis_query, basis_output, gram)
 
 
 def body(tokens, segments, norm_gain, q_weight, kv_weight, o_weight, basis_query, basis_output):
@@ -125,20 +570,15 @@
     output_scale = qwidth ** (-0.5)
     gn_scale = qwidth / (row_count * groups)
     param_count = 2.0 * D * qwidth
-    normed = rms_normed(tokens, norm_gain)
-    dir_query = basis_query[K - 1]
     dir_output = basis_output[K - 1]
-    kv_head = lax.axis_index(TENSOR) * heads_dev // group_size
-    kv_columns = lax.dynamic_slice_in_dim(kv_weight, kv_head * HD, HD, 2)
-    kv_pair = jnp.concatenate([kv_columns[0], kv_columns[1]], axis=1)
-    pieces = sent_together((q_weight, dir_query, kv_pair), DP, 0, 1)
-    sum_query = jnp.dot(normed, pieces[0], preferred_element_type=jnp.float32)
-    sum_tangent = jnp.dot(normed, pieces[1], preferred_element_type=jnp.float32)
-    sum_pair = jnp.dot(normed, pieces[2], preferred_element_type=jnp.float32)
-    query = sum_query.astype(jnp.bfloat16)
-    tangent = (sum_tangent * query_scale).astype(jnp.bfloat16)
-    key_states = sum_pair[:, :HD].astype(jnp.bfloat16)
-    values = sum_pair[:, HD:].astype(jnp.bfloat16)
+    query, tangent, key_states, values, normed, gram = project(
+        tokens.reshape(row_count, model_width),
+        norm_gain.reshape(1, model_width),
+        q_weight,
+        basis_query,
+        kv_weight,
+        basis_output,
+    )
     allowed = allowed_pairs(segments)
     query_wide = query.astype(jnp.float32).reshape(seq_count, length, heads_dev, HD)
     tangent_wide = tangent.astype(jnp.float32).reshape(seq_count, length, heads_dev, HD)
@@ -170,60 +610,11 @@
     _, pullback = jax.vjp(attend_here, query_wide)
     cot_query = pullback(cot_heads.reshape(seq_count, length, heads_dev, HD))[0]
     cot_query = cot_query.reshape(row_count, col_count).astype(jnp.bfloat16)
-    gn_query = lax.psum_scatter(
-        (
-            lax.dot_general(
-                normed, cot_query, (((0,), (0,)), ((), ())), preferred_element_type=jnp.float32
-            )
-            * (gn_scale * query_scale)
-        ).astype(jnp.bfloat16),
-        DP,
-        scatter_dimension=0,
-        tiled=True,
-    ).astype(jnp.float32)
-
-    def local_products(vec_query, vec_output):
-        return jnp.sum(basis_query.astype(jnp.float32) * vec_query[None], axis=(1, 2)) + jnp.sum(
-            basis_output.astype(jnp.float32) * vec_output[None], axis=(1, 2)
-        )
-
-    def remove(vec_query, vec_output, weights_now):
-        return (
-            vec_query
-            - jnp.sum(weights_now[:, None, None] * basis_query.astype(jnp.float32), axis=0),
-            vec_output
-            - jnp.sum(weights_now[:, None, None] * basis_output.astype(jnp.float32), axis=0),
-        )
-
-    local_gram = jnp.einsum(
-        "kab,lab->kl", basis_query, basis_query, preferred_element_type=jnp.float32
-    ) + jnp.einsum("kab,lab->kl", basis_output, basis_output, preferred_element_type=jnp.float32)
-    first_sum, gram_sum = (
-        one_axis_at_a_time(local_products(gn_query, gn_output), DP_TENSOR),
-        one_axis_at_a_time(local_gram, DP_TENSOR),
-    )
-    first_coeffs = first_sum / param_count
-    gram_matrix = gram_sum / param_count
-    kept_query, kept_output = remove(gn_query, gn_output, first_coeffs)
-    kept_squares = jnp.sum(kept_query * kept_query) + jnp.sum(kept_output * kept_output)
-    second_sum, kept_sum = (
-        one_axis_at_a_time(local_products(kept_query, kept_output), DP_TENSOR),
-        one_axis_at_a_time(kept_squares, DP_TENSOR),
-    )
-    second_coeffs = second_sum / param_count
-    clean_query, clean_output = remove(kept_query, kept_output, second_coeffs)
-    squares = (
-        kept_sum / param_count
-        - 2.0 * jnp.sum(second_coeffs * second_coeffs)
-        + jnp.sum(second_coeffs[:, None] * gram_matrix * second_coeffs[None, :])
-    )
-    beta = jnp.sqrt(squares + BETA_EPS)
-    coefficients = jnp.concatenate([first_coeffs + second_coeffs, beta[None]])
-    return (
-        (clean_query / beta).astype(jnp.bfloat16),
-        (clean_output / beta).astype(jnp.bfloat16),
-        coefficients,
-    )
+    gn_query = query_grad(normed, cot_query.T, gn_scale * query_scale)
+    next_query, next_output, lines = clean(
+        gn_query, gn_output, basis_query, basis_output, gram, param_count
+    )
+    return (next_query, next_output, lines[:9, 0])
 
 
 def solution(mesh):

time: 747 us -> 536 us (0.72); the launches traced: 738 us -> 535 us
  waiting for transfers between devices: 490 us -> 285 us
  Pallas kernels: 0 us -> 173 us
  blocking collectives: 69 us -> 0 us
  other arithmetic: 65 us -> 6.15 us
  matrix products: 83.3 us -> 39.5 us
    pallas_call x0 -> x3, Pallas kernels: none -> 173 us  [the longest x1 87.3 us: project(): pl.pallas_call(project_kernel, out_shape=(shape((512, 256), BF), shape((5...]
    all_gather x2 -> x1, waiting for transfers between devices: 203 us -> 71 us  [sent_together(): lax.all_gather(both, axis, axis=dim, tiled=True)]
    reduce_scatter x1 -> x0, waiting for transfers between devices: 74.3 us -> none  [body(): lax.psum_scatter((lax.dot_general(normed, cot_query, (((0,), (0,)), ((),...]
    psum x10 -> x0, blocking collectives: 69 us -> none  [one_axis_at_a_time(): value = lax.psum(value, axis)]
    dot_general x6 -> x0, matrix products: 42.7 us -> none  [the longest x1 8.96 us: body(): jnp.einsum('kab,lab->kl', basis_query, basis_query, preferred_element_typ...]
    reduce_sum x12 -> x0, other arithmetic: 30.1 us -> none  [the longest x2 7.99 us: remove(): jnp.sum(weights_now[:, None, None] * basis_output.astype(jnp.float32), ax...]
    convert_element_type x5 -> x0, other arithmetic: 25.9 us -> none  [the longest x2 20.4 us: rms_normed(): return (flat_rows * inv_rms * norm_gain[None, :]).astype(jnp.bfloat16)]
  transfers between devices with their start and end apart: 6 -> 4, of which waited for: 6 -> 4; matrix products, arithmetic and copies ran while one was open for 5% -> 1% of each run, Pallas kernels for 0% -> 0%
where the time goes in v1:
time: 536 us; the launch traced here: 535 us
  waiting for transfers between devices  285 us (53%)
  Pallas kernels  173 us (32%)
  matrix products  39.5 us (7%)
  local copies, waits for them, and re-layouts  16.3 us (3%)
  between operations  14 us (3%)
  other arithmetic  6.15 us (1%)
    reduce_scatter x1, waiting for transfers between devices, total_of(): lax.psum_scatter(filled_up(lines, lax.axis_size(axis)), axis, scatter_dim...  94.6 us
    pallas_call x1, Pallas kernels, project(): pl.pallas_call(project_kernel, out_shape=(shape((512, 256), BF), shape((5...  87.3 us
    all_gather x1, waiting for transfers between devices, sent_together(): lax.all_gather(both, axis, axis=dim, tiled=True)  71 us
    reduce_scatter x1, waiting for transfers between devices, body(): lax.psum_scatter(lax.dot_general(tangent_columns, o_weight, (((1,), (1,))...  65 us
    all_gather x1, waiting for transfers between devices, total_of(): whole = lax.all_gather(own, axis).reshape(-1, *lines.shape[1:])  54.7 us
    pallas_call x1, Pallas kernels, clean(): pl.pallas_call(functools.partial(clean_kernel, count), out_shape=(shape((...  44.7 us
    pallas_call x1, Pallas kernels, query_grad(): pl.pallas_call(functools.partial(query_grad_kernel, factor), out_shape=ja...  41.5 us
  transfers between devices with their start and end apart: 4, of which 4 were waited for; matrix products, arithmetic and copies ran while one was open for 1% of the time, Pallas kernels for 0%

profile of v1, /device:TPU:1, one launch (start us, length us, event | category | flops | bytes accessed | tf_op | source)
XLA Modules:
  0.0 535.2 jit_solution(7183064987065157737)
XLA Ops:
  7.2 0.0 copy-start
  7.2 0.0 all-gather.4.cloned.1.call-start
  7.3 87.3 %project.1 = (bf16[512,256]{1,0:T(8,128)(2,1)}, bf16[512,256]{1,0:T(8,128)(2,1)}, bf16[512,128]{1,0:T(8,128)(2,1)}, bf16[512,128]{1,0:T(8,128)(2,1)}, bf16[512,8192]{1,0:T(8,128)(2,1)}, /*index=5*/f32[64,128]{1,0:T(8,128)}) custom-call(bf16[512,8192]{1,0:T(8,128)(2,1)} %bitcast.106, f32[1,8192]{1,0:T(1,128)} %bitcast.118, bf16[1024,256]{1,0:T(8,128)(2,1)} %q_w.1, ...), custom_call_target="tpu_custom_call" | custom-call | tf_op jit(solution)/shard_map/project/pallas_call | solution.py:329
  94.6 0.0 copy-start.7
  94.6 1.2 reshape.185
  95.8 1.2 reshape.187
  97.1 0.5 fusion.41
  97.6 0.9 convert.3
  98.5 1.1 fusion.51
  99.6 0.2 multiply_subtract_fusion.2
  99.8 0.0 copy-done.7
  99.8 0.9 compare_and_fusion.1
  100.7 0.2 multiply_subtract_fusion.1
  101.0 1.2 fusion.17
  102.2 0.2 fusion.42
  102.5 0.0 copy-done.4
  102.5 1.4 fusion.4
  103.9 1.8 copy.30
  105.7 1.7 copy.75
  107.5 1.4 fusion.53
  108.8 0.0 copy-start.2
  108.9 0.0 copy-done.5
  108.9 0.8 fusion.5
  109.7 0.2 copy.35
  109.9 0.0 copy-done.2
  110.0 0.8 pad_maximum_fusion
  110.8 0.0 all-gather.4.cloned.1.call-update
  110.8 0.2 reduce-scatter.3.cloned.1.call-start
  111.0 71.0 %all-gather.4.cloned.1.call-done = bf16[4096,512]{1,0:T(8,128)(2,1)} async-done(((bf16[512,512]{1,0:T(8,128)(2,1)}), bf16[4096,512]{1,0:T(8,128)(2,1)}) %all-gather.4.cloned.1.call-update) | async-done | bytes 4194320 | tf_op jit(solution)/shard_map/all_gather | solution.py:92
  182.1 9.9 %fusion.24 = f32[4096,1024]{1,0:T(8,128)} fusion(bf16[8,256,1024]{2,1,0:T(8,128)(2,1)} %vo.1, bf16[4096,512]{1,0:T(8,128)(2,1)} %all-gather.4.cloned.1.call-done), kind=kOutput, calls=%fused_computation.36 | convolution fusion | flops 2147483648 | bytes 19398656 | tf_op jit(solution)/shard_map/dot_general | solution.py:595
  192.0 0.0 copy-done
  192.0 0.0 copy-done.1
  192.0 9.3 %add_convert_fusion = bf16[4096,1024]{1,0:T(8,128)(2,1)} fusion(f32[4096,1024]{1,0:T(8,128)} %fusion.24, bf16[256,1024]{1,0:T(8,128)(2,1)S(1)} %copy-done, bf16[4096,512]{1,0:T(8,128)(2,1)S(1)} %copy-done.1), kind=kOutput, calls=%fused_computation | convolution fusion | flops 2160066560 | bytes 27787264 | tf_op jit(solution)/shard_map/dot_general | solution.py:597
  201.2 0.0 reduce-scatter.3.cloned.1.call-update
  201.3 0.0 all-gather.6.cloned.1.call-start
  201.3 94.6 %reduce-scatter.3.cloned.1.call-done = bf16[256,1024]{1,0:T(8,128)(2,1)} async-done(((bf16[4096,1024]{1,0:T(8,128)(2,1)}), bf16[256,1024]{1,0:T(8,128)(2,1)}) %reduce-scatter.3.cloned.1.call-update) | async-done | bytes 524304 | tf_op jit(solution)/shard_map/reduce_scatter | solution.py:102
  295.9 0.0 all-gather.6.cloned.1.call-update
  295.9 0.0 copy-start.3
  295.9 0.0 reduce-scatter.5.cloned.1.call-start
  295.9 54.7 %all-gather.6.cloned.1.call-done = bf16[4096,1024]{1,0:T(8,128)(2,1)} async-done(((bf16[256,1024]{1,0:T(8,128)(2,1)}), bf16[4096,1024]{1,0:T(8,128)(2,1)}) %all-gather.6.cloned.1.call-update) | async-done | bytes 8388624 | tf_op jit(solution)/shard_map/all_gather | solution.py:105
  350.7 7.1 %convolution_convert_fusion = bf16[4096,256]{1,0:T(8,128)(2,1)} fusion(bf16[4096,1024]{1,0:T(8,128)(2,1)} %all-gather.6.cloned.1.call-done, bf16[256,1024]{1,0:T(8,128)(2,1)S(1)} %copy-done), kind=kOutput, calls=%fused_computation.3 | convolution fusion | flops 2148532224 | bytes 11010048 | tf_op jit(solution)/shard_map/dot_general | solution.py:602
  357.8 0.0 reduce-scatter.5.cloned.1.call-update
  357.8 0.0 copy-done.3
  357.8 0.3 copy.25
  358.1 0.0 slice-start
  358.1 1.6 slice-done
  359.7 5.8 %multiply_convert_fusion = bf16[8,256,1024]{2,1,0:T(8,128)(2,1)S(1)} fusion(bf16[8,512,256]{2,1,0:T(8,128)(2,1)S(1)} %bitcast.105, bf16[8,512,1024]{2,1,0:T(8,128)(2,1)} %bitcast.120), kind=kOutput, calls=%fused_computation.2 | convolution fusion | flops 2151677952 | bytes 14680064 | tf_op jit(solution)/shard_map/nta,ntb->nab/dot_general | solution.py:158
  365.5 0.0 copy-start.6
  365.5 1.8 convert_reduce_fusion.go
  367.3 65.0 %reduce-scatter.5.cloned.1.call-done = bf16[512,256]{1,0:T(8,128)(2,1)} async-done(((bf16[4096,256]{1,0:T(8,128)(2,1)}), bf16[512,256]{1,0:T(8,128)(2,1)}) %reduce-scatter.5.cloned.1.call-update) | async-done | bytes 262160 | tf_op jit(solution)/shard_map/reduce_scatter | solution.py:601
  432.3 1.0 reshape.179
  433.3 0.1 copy.36
  433.5 0.0 copy-done.6
  433.5 0.4 multiply_reduce_fusion
  433.9 2.1 fusion.15
  436.0 0.2 multiply_add_fusion.1
  436.3 0.2 add_convert_fusion.1
  436.5 0.2 copy.40
  436.7 0.7 copy.63
  437.4 41.5 %query_grad.1.gq = f32[1024,256]{1,0:T(8,128)} custom-call(bf16[512,8192]{1,0:T(8,128)(2,1)} %get-tuple-element.12.normed, bf16[256,512]{1,0:T(8,128)(2,1)} %bitcast.107), custom_call_target="tpu_custom_call" | custom-call | tf_op jit(solution)/shard_map/query_grad/pallas_call | solution.py:420
  478.9 44.7 %clean.1 = (bf16[1024,256]{1,0:T(8,128)(2,1)}, bf16[256,1024]{1,0:T(8,128)(2,1)}, f32[16,128]{1,0:T(8,128)}) custom-call(f32[1024,256]{1,0:T(8,128)} %query_grad.1.gq, f32[256,1024]{1,0:T(8,128)} %convert_reduce_fusion.go, bf16[8,1024,256]{2,1,0:T(8,128)(2,1)} %vq.1, bf16[8,256,1024]{2,1,0:T(8,128)(2,1)} %vo.1, f32[64,128]{1,0:T(8,128)} %get-tuple-element.17.gram), custom_call_target="tpu_custom_call" | custom-call | tf_op jit(solution)/shard_map/clean/pallas_call | solution.py:539
  523.6 1.3 slice_reduce_fusion
  524.9 1.9 copy.78
  526.8 1.9 copy.79
  (9 shorter events, 0.1 us)
Async XLA Ops:
  7.2 184.8 %copy-start = (bf16[256,1024]{1,0:T(8,128)(2,1)S(1)}, bf16[256,1024]{1,0:T(8,128)(2,1)}, u32[]{:S(2)}) copy-start(bf16[256,1024]{1,0:T(8,128)(2,1)} %param.13) | copy-start | bytes 1572868
  7.2 174.9 %all-gather.4.cloned.1.call-start = ((), (), s32[]{:S(2)}) async-start(), calls=%async_computation.2 | async-start | bytes 4718592 | tf_op jit(solution)/shard_map/all_gather | solution.py:92
  94.6 5.2 copy-start.7
  100.7 1.7 copy-start.4
  105.7 3.1 copy-start.5
  108.8 1.1 copy-start.2
  110.8 185.1 %reduce-scatter.3.cloned.1.call-start = ((), (), s32[]{:S(2)}) async-start(), calls=%async_computation.3 | async-start | bytes 8912896 | tf_op jit(solution)/shard_map/reduce_scatter | solution.py:102
  182.1 9.9 %copy-start.1 = (bf16[4096,512]{1,0:T(8,128)(2,1)S(1)}, bf16[4096,512]{1,0:T(8,128)(2,1)}, u32[]{:S(2)}) copy-start(bf16[4096,512]{1,0:T(8,128)(2,1)} %all-gather.4.cloned.1.call-done) | copy-start | bytes 12582916
  201.3 149.4 %all-gather.6.cloned.1.call-start = ((), (), s32[]{:S(2)}) async-start(), calls=%async_computation.5 | async-start | bytes 8912896 | tf_op jit(solution)/shard_map/all_gather | solution.py:105
  295.9 61.9 %copy-start.3 = (pred[2,256,256]{1,2,0:T(8,128)(4,1)S(1)}, pred[2,256,256]{1,2,0:T(8,128)(4,1)}, u32[]{:S(2)}) copy-start(pred[2,256,256]{1,2,0:T(8,128)(4,1)} %get-tuple-element.35) | copy-start | bytes 393220
  295.9 136.4 %reduce-scatter.5.cloned.1.call-start = ((), (), s32[]{:S(2)}) async-start(), calls=%async_computation.4 | async-start | bytes 2359296 | tf_op jit(solution)/shard_map/reduce_scatter | solution.py:601
  358.1 1.6 slice-start
  365.5 68.0 %copy-start.6 = (bf16[512,128]{1,0:T(8,128)(2,1)S(1)}, bf16[512,128]{1,0:T(8,128)(2,1)}, u32[]{:S(2)}) copy-start(bf16[512,128]{1,0:T(8,128)(2,1)} %get-tuple-element.13) | copy-start | bytes 393220
Sparse Core Ops, SparseCore 0:
  110.9 71.0 all-gather.3
  201.4 94.4 reduce-scatter.2
  297.6 53.0 all-gather.5
  357.9 74.3 reduce-scatter.4

commit v2 on v1

--- a/solution.py
+++ b/solution.py
@@ -81,29 +81,25 @@
 
 
 STAGES = ((X1, YH, X3), (X3, YH, X1))
-
-
-def sent_together(arrays, axis, dim, along):
-    ends, at = ([], 0)
-    for a in arrays[:-1]:
-        at += a.shape[along]
-        ends.append(at)
-    both = jnp.concatenate(arrays, axis=along)
-    return tuple(jnp.split(lax.all_gather(both, axis, axis=dim, tiled=True), ends, axis=along))
-
-
-def filled_up(lines, count):
-    spare = -len(lines) % count
-    return jnp.pad(lines, [(0, spare)] + [(0, 0)] * (lines.ndim - 1))
-
-
-def total_of(value, axis):
-    lines = value.reshape(-1, *value.shape[1:][-1:])
-    own = lax.psum_scatter(
-        filled_up(lines, lax.axis_size(axis)), axis, scatter_dimension=0, tiled=True
-    )
-    whole = lax.all_gather(own, axis).reshape(-1, *lines.shape[1:])
-    return lax.slice_in_dim(whole, 0, len(lines)).reshape(value.shape)
+OUT_STAGES = ((YL, Z1, Z3, CORE), (YL, Z3, Z1, CORE))
+
+
+DP_PEERS = [(x, yh, 0, 0, 0) for x in range(4) for yh in range(2) if x or yh]
+TENSOR_PEERS = [(0, 0, z, yl, c) for z in range(4) for yl in range(2) for c in range(2) if z or yl or c]
+
+
+def z_place(mask, kind):
+    one, three = {0: (0, 0), 1: (1, 0), 3: (0, 1), 2: (1, 1)}[mask]
+    return one + 2 * three if kind == 0 else three + 2 * one
+
+
+def out_place(r, kind):
+    mz, ml, mc = r // 4, r // 2 % 2, r % 2
+    return ml + 2 * z_place(mz, kind) + 8 * mc
+
+
+def tensor_masks(r):
+    return (0, 0, r // 4, r // 2 % 2, r % 2)
 
 
 def rope_tables(length, head_width):
@@ -151,24 +147,13 @@
     return jnp.logical_and(segments[:, :, None] == segments[:, None, :], causal[None])
 
 
-def block_products(left_rows, right_rows, block_count, factor):
-    left_blocks = left_rows.reshape(block_count, -1, left_rows.shape[1])
-    right_blocks = right_rows.reshape(block_count, -1, right_rows.shape[1])
-    terms = (
-        jnp.einsum("nta,ntb->nab", left_blocks, right_blocks, preferred_element_type=jnp.float32)
-        * factor
-    )
-    rounded = lax.optimization_barrier(terms.astype(jnp.bfloat16))
-    return jnp.sum(rounded.astype(jnp.float32), axis=0)
-
-
 SUPER = (0, 1, 0, 1, 2, 3, 2, 3)
 HALF = (0, 0, 1, 1, 0, 0, 1, 1)
 
 
 def project_kernel(
-    tok, gain, q_w, vec_q, kv_w, vec_o,
-    q_out, t_out, k_out, v_out, normed_out, gram_out,
+    tok, gain, q_w, vec_q, kv_w, vec_o, o_w,
+    q_out, t_out, k_out, v_out, normed_out, gram_out, wall,
     x, buf, acc, mine, theirs, vq, vo, load, sent, got,
 ):
     here = position()
@@ -187,13 +172,18 @@
             copy = pltpu.make_async_copy(src, dst, load.at[3 * s + n])
             copy.start()
             for_rows.append(copy)
+    own_out = []
+    for kind, src in enumerate((vec_o.at[K - 1], o_w)):
+        copy = pltpu.make_async_copy(src, wall.at[kind, 0], load.at[16 + kind])
+        copy.start()
+        own_out.append(copy)
     tok_copy = pltpu.make_async_copy(tok, x, load.at[12])
     tok_copy.start()
     vq_copy = pltpu.make_async_copy(vec_q, vq, load.at[13])
     vq_copy.start()
     vo_copy = pltpu.make_async_copy(vec_o, vo, load.at[14])
     vo_copy.start()
-    greet(here, (X1, X3, YH, CORE))
+    greet(here, (X1, X3, YH, CORE, Z1, Z3, YL))
     for copy in for_rows:
         copy.wait()
 
@@ -211,6 +201,31 @@
         )
 
     first = [start_stage(0, k) for k in range(8)]
+    out_copies = {}
+
+    def start_out(stage, kind, half):
+        n = 1 << stage
+        rows = pl.ds(half * 128, 128)
+        at = 25 + stage * 4 + kind * 2 + half
+        out_copies[stage, kind, half] = send(
+            wall.at[kind, pl.ds(0, n), rows],
+            wall.at[kind, pl.ds(n, n), rows],
+            sent.at[at],
+            got.at[at],
+            here,
+            OUT_STAGES[kind][stage],
+        )
+
+    def next_out(stage, half):
+        for kind in range(2):
+            out_copies[stage, kind, half].wait_recv()
+            start_out(stage + 1, kind, half)
+
+    for copy in own_out:
+        copy.wait()
+    for half in range(2):
+        for kind in range(2):
+            start_out(0, kind, half)
 
     def norm_rows(lo, hi):
         def step(i, carry):
@@ -288,6 +303,14 @@
             vq_copy.wait()
             vo_copy.wait()
             gram()
+        if k < 2:
+            next_out(0, k)
+        if k == 2:
+            next_out(1, 0)
+        if k == 4:
+            next_out(1, 1)
+        if k == 6:
+            next_out(2, 0)
         if k == 4:
             dots(0, 0, 4)
         if k == 5:
@@ -296,6 +319,7 @@
             dots(2, 0, 4)
     second[7].wait_recv()
     third.append(start_stage(2, 7))
+    next_out(2, 1)
     dots(3, 0, 4)
     for s, (k0, k1) in enumerate(((0, 2), (1, 3), (4, 6), (5, 7))):
         third[k0].wait_recv()
@@ -313,6 +337,10 @@
     v_out[...] = jnp.where(first_core, other, own).astype(BF)
     for copy in first + second + third:
         copy.wait_send()
+    for (stage, kind, half), copy in out_copies.items():
+        copy.wait_send()
+        if stage == 3:
+            copy.wait_recv()
     out_copy.wait()
 
 
@@ -324,7 +352,7 @@
     return [pl.BlockSpec(memory_space=pltpu.VMEM) for _ in range(n)]
 
 
-def project(tokens, norm_gain, q_weight, basis_query, kv_weight, basis_output):
+def project(tokens, norm_gain, q_weight, basis_query, kv_weight, basis_output, o_weight):
     shape = jax.ShapeDtypeStruct
     return pl.pallas_call(
         project_kernel,
@@ -335,9 +363,10 @@
             shape((512, HD), BF),
             shape((512, D), BF),
             shape((64, 128), F32),
+            shape((2, 16, 256, 1024), BF),
         ),
-        in_specs=any_specs(1) + vmem_specs(1) + any_specs(4),
-        out_specs=tuple(vmem_specs(4) + any_specs(1) + vmem_specs(1)),
+        in_specs=any_specs(1) + vmem_specs(1) + any_specs(5),
+        out_specs=tuple(vmem_specs(4) + any_specs(1) + vmem_specs(1) + any_specs(1)),
         scratch_shapes=[
             pltpu.VMEM((512, D), BF),
             pltpu.VMEM((4, 8, 256, 640), BF),
@@ -346,21 +375,254 @@
             pltpu.VMEM((512, HD), BF),
             pltpu.VMEM((K, 1024, 256), BF),
             pltpu.VMEM((K, 256, 1024), BF),
-            pltpu.SemaphoreType.DMA((16,)),
-            pltpu.SemaphoreType.DMA((25,)),
-            pltpu.SemaphoreType.DMA((25,)),
+            pltpu.SemaphoreType.DMA((18,)),
+            pltpu.SemaphoreType.DMA((41,)),
+            pltpu.SemaphoreType.DMA((41,)),
         ],
         compiler_params=pltpu.CompilerParams(
             collective_id=0, has_side_effects=True, vmem_limit_bytes=VMEM_BYTES
         ),
         name="project",
-    )(tokens, norm_gain, q_weight, basis_query, kv_weight, basis_output)
-
-
-def query_grad_kernel(factor, normed, cot, out, part, r1, r2, r3, sent, got):
+    )(tokens, norm_gain, q_weight, basis_query, kv_weight, basis_output, o_weight)
+
+
+def output_kernel(
+    h, wall, cot, gp_out,
+    w, g, acc, tb, cs, c1, c2, c3, gp, load, sent, got,
+):
     here = position()
-    greet(here, (X1, X3, YH))
+    tensor = here[2] * 4 + here[3] * 2 + here[4]
+    loads = []
+    for kind in (0, 1):
+        copy = pltpu.make_async_copy(wall.at[kind], w.at[kind], load.at[kind])
+        copy.start()
+        loads.append(copy)
+    greet(here, [X1, X3, YH] + TENSOR_PEERS)
     copies = []
+
+    def start(at, src, dst, masks):
+        copy = send(src, dst, sent.at[at], got.at[at], here, masks)
+        copies.append(copy)
+        return copy
+
+    def index_of(r):
+        z, yl, c = peer(here[2:], tensor_masks(r)[2:])
+        return z * 4 + yl * 2 + c
+
+    spread = {
+        r: start(r, h.at[index_of(r)], g.at[:, r, 0], tensor_masks(r)) for r in range(1, 16)
+    }
+    g[:, 0, 0] = h[tensor]
+
+    def gather(stage, rg, kind):
+        n = 1 << stage
+        group = pl.ds(rg * 4, 4)
+        return start(
+            16 + stage * 8 + rg * 2 + kind,
+            g.at[kind, group, pl.ds(0, n)],
+            g.at[kind, group, pl.ds(n, n)],
+            STAGES[kind][stage],
+        )
+
+    one, two, three = {}, {}, {}
+    for rg in range(4):
+        for r in range(rg * 4, rg * 4 + 4):
+            if r:
+                spread[r].wait_recv()
+        for kind in range(2):
+            one[rg, kind] = gather(0, rg, kind)
+    order = [(rg, kind) for rg in range(4) for kind in range(2)]
+    for n, key in enumerate(order):
+        one[key].wait_recv()
+        two[key] = gather(1, *key)
+        if n >= 1:
+            two[order[n - 1]].wait_recv()
+            three[order[n - 1]] = gather(2, *order[n - 1])
+    two[order[7]].wait_recv()
+    three[order[7]] = gather(2, *order[7])
+
+    def rows_of(r, cols):
+        parts = [g[kind, r, :, :, cols].reshape(128, 256) for kind in range(2)]
+        return jnp.concatenate(parts, axis=0)
+
+    for copy in loads:
+        copy.wait()
+    acc[...] = jnp.zeros_like(acc)
+    for rg in range(4):
+        three[rg, 0].wait_recv()
+        three[rg, 1].wait_recv()
+        for r in range(rg * 4, rg * 4 + 4):
+            acc[...] += jnp.dot(
+                rows_of(r, pl.ds(0, 256)), w[0, out_place(r, 0)], preferred_element_type=F32
+            ) + jnp.dot(
+                rows_of(r, pl.ds(256, 256)), w[1, out_place(r, 1)], preferred_element_type=F32
+            )
+    tb[...] = acc[...].astype(BF)
+
+    def scatter(stage, key, src, dst):
+        rg, kind = key
+        return start(40 + stage * 8 + rg * 2 + kind, src, dst, STAGES[kind][2 - stage])
+
+    one, two, three = {}, {}, {}
+    for rg in range(4):
+        group = pl.ds(rg * 4, 4)
+        for r in range(rg * 4, rg * 4 + 4):
+            part = lax.dot_general(
+                tb[...],
+                w[1, out_place(r, 1)],
+                (((1,), (1,)), ((), ())),
+                preferred_element_type=F32,
+            ).astype(BF)
+            for kind in range(2):
+                cs[kind, r] = part[kind * 128 : kind * 128 + 128].reshape(8, 16, 256)
+        for kind in range(2):
+            one[rg, kind] = scatter(
+                0, (rg, kind), cs.at[kind, group, pl.ds(4, 4)], c1.at[kind, group]
+            )
+
+    def added(key, n, ref):
+        rg, kind = key
+        group = pl.ds(rg * 4, 4)
+        cs[kind, group, pl.ds(0, n)] = (
+            cs[kind, group, pl.ds(0, n)].astype(F32) + ref[kind, group].astype(F32)
+        ).astype(BF)
+
+    def output_grad(r):
+        mz, ml, mc = r // 4, r // 2 % 2, r % 2
+        block = lax.dot_general(
+            rows_of(r, pl.ds(0, 256)),
+            tb[...],
+            (((0,), (0,)), ((), ())),
+            preferred_element_type=F32,
+        ).astype(BF)
+        for kind in range(2):
+            gp[mc, kind, z_place(mz, kind), ml] = block[:, kind * 512 : kind * 512 + 512]
+
+    def second(key):
+        rg, kind = key
+        one[key].wait_recv()
+        added(key, 4, c1)
+        group = pl.ds(rg * 4, 4)
+        two[key] = scatter(1, key, cs.at[kind, group, pl.ds(2, 2)], c2.at[kind, group])
+
+    def third(key):
+        rg, kind = key
+        two[key].wait_recv()
+        added(key, 2, c2)
+        group = pl.ds(rg * 4, 4)
+        three[key] = scatter(2, key, cs.at[kind, group, pl.ds(1, 1)], c3.at[kind, group])
+
+    for n, key in enumerate(order):
+        second(key)
+        if n >= 1:
+            third(order[n - 1])
+        output_grad(2 * n)
+        output_grad(2 * n + 1)
+    third(order[7])
+    back = {}
+    for rg in range(4):
+        for kind in range(2):
+            three[rg, kind].wait_recv()
+            added((rg, kind), 1, c3)
+        for r in range(rg * 4, rg * 4 + 4):
+            if r:
+                back[r] = start(64 + r, cs.at[:, r, 0], cot.at[tensor], tensor_masks(r))
+    cot[tensor] = cs[:, 0, 0]
+    gp_copy = pltpu.make_async_copy(gp, gp_out, load.at[2])
+    gp_copy.start()
+    for r in range(1, 16):
+        back[r].wait_recv()
+    for copy in copies:
+        copy.wait_send()
+    gp_copy.wait()
+
+
+def output_side(heads, wall):
+    shape = jax.ShapeDtypeStruct
+    return pl.pallas_call(
+        output_kernel,
+        out_shape=(shape((16, 2, 16, 256), BF), shape((2, 2, 4, 2, 256, 512), BF)),
+        in_specs=vmem_specs(1) + any_specs(1),
+        out_specs=tuple(vmem_specs(1) + any_specs(1)),
+        scratch_shapes=[
+            pltpu.VMEM((2, 16, 256, 1024), BF),
+            pltpu.VMEM((2, 16, 8, 16, 512), BF),
+            pltpu.VMEM((256, 1024), F32),
+            pltpu.VMEM((256, 1024), BF),
+            pltpu.VMEM((2, 16, 8, 16, 256), BF),
+            pltpu.VMEM((2, 16, 4, 16, 256), BF),
+            pltpu.VMEM((2, 16, 2, 16, 256), BF),
+            pltpu.VMEM((2, 16, 1, 16, 256), BF),
+            pltpu.VMEM((2, 2, 4, 2, 256, 512), BF),
+            pltpu.SemaphoreType.DMA((3,)),
+            pltpu.SemaphoreType.DMA((80,)),
+            pltpu.SemaphoreType.DMA((80,)),
+        ],
+        compiler_params=pltpu.CompilerParams(
+            collective_id=3, has_side_effects=True, vmem_limit_bytes=VMEM_BYTES
+        ),
+        name="output_side",
+    )(heads, wall)
+
+
+def grads_kernel(
+    factor, normed, cot, gp, out_q, out_o,
+    part, r1, r2, r3, own, rc, z1, z2, y1, load, sent, got,
+):
+    here = position()
+    load_own = pltpu.make_async_copy(gp.at[0], own, load.at[0])
+    load_own.start()
+    greet(here, (X1, X3, YH, CORE, Z1, Z3, YL))
+    copies = []
+
+    def keep(copy):
+        copies.append(copy)
+        return copy
+
+    def rows_at(j):
+        return pl.ds(j // 2 * 64, 64)
+
+    def start_out(stage, j, src, dst):
+        at = 24 + stage * 8 + j
+        masks = (CORE, (Z3, Z1)[j % 2], (Z1, Z3)[j % 2], YL)[stage]
+        return keep(send(src, dst, sent.at[at], got.at[at], here, masks))
+
+    over_core = [
+        start_out(0, j, gp.at[1, j % 2, :, :, rows_at(j)], rc.at[j % 2, :, :, rows_at(j)])
+        for j in range(8)
+    ]
+    z_high, z_low, over_y = {}, {}, {}
+
+    def out_high(j):
+        kind, rows = j % 2, rows_at(j)
+        over_core[j].wait_recv()
+        own[kind, :, :, rows] = (
+            own[kind, :, :, rows].astype(F32) + rc[kind, :, :, rows].astype(F32)
+        ).astype(BF)
+        z_high[j] = start_out(1, j, own.at[kind, pl.ds(2, 2), :, rows], z1.at[kind, :, :, rows])
+
+    def out_low(j):
+        kind, rows = j % 2, rows_at(j)
+        z_high[j].wait_recv()
+        own[kind, pl.ds(0, 2), :, rows] = (
+            own[kind, pl.ds(0, 2), :, rows].astype(F32) + z1[kind, :, :, rows].astype(F32)
+        ).astype(BF)
+        z_low[j] = start_out(2, j, own.at[kind, 1, :, rows], z2.at[kind, :, rows])
+
+    def out_y(j):
+        kind, rows = j % 2, rows_at(j)
+        z_low[j].wait_recv()
+        own[kind, 0, :, rows] = (
+            own[kind, 0, :, rows].astype(F32) + z2[kind, :, rows].astype(F32)
+        ).astype(BF)
+        over_y[j] = start_out(3, j, own.at[kind, 0, 1, rows], y1.at[kind, rows])
+
+    def out_end(j):
+        kind, rows = j % 2, rows_at(j)
+        over_y[j].wait_recv()
+        out_o[rows, pl.ds(kind * 512, 512)] = own[kind, 0, 0, rows].astype(F32) + y1[
+            kind, rows
+        ].astype(F32)
 
     def product(low, mid, high):
         source = dp_source(here, low, mid, high, 0)
@@ -373,9 +635,7 @@
 
     def start(stage, c, src, dst):
         at = stage * 8 + c
-        copy = send(src, dst, sent.at[at], got.at[at], here, STAGES[c % 2][2 - stage])
-        copies.append(copy)
-        return copy
+        return keep(send(src, dst, sent.at[at], got.at[at], here, STAGES[c % 2][2 - stage]))
 
     def start_first(c):
         return start(0, c, part.at[c, pl.ds(4, 4)], r1.at[c])
@@ -385,9 +645,12 @@
     product(0, 0, 1)
     product(0, 1, 1)
     one = {c: start_first(c) for c in (0, 2, 4, 6)}
+    load_own.wait()
+    out_high(0)
     product(1, 0, 0)
     product(1, 1, 0)
     one.update({c: start_first(c) for c in (1, 3, 5, 7)})
+    out_high(1)
     product(0, 0, 0)
     product(0, 1, 0)
 
@@ -397,48 +660,63 @@
         ).astype(BF)
 
     two, three = {}, {}
-    for c in range(8):
+
+    def q_two(c):
         one[c].wait_recv()
         added(c, 4, r1)
         two[c] = start(1, c, part.at[c, pl.ds(2, 2)], r2.at[c])
-        if c >= 1:
-            two[c - 1].wait_recv()
-            added(c - 1, 2, r2)
-            three[c - 1] = start(2, c - 1, part.at[c - 1, pl.ds(1, 1)], r3.at[c - 1])
-    two[7].wait_recv()
-    added(7, 2, r2)
-    three[7] = start(2, 7, part.at[7, pl.ds(1, 1)], r3.at[7])
-    for c in range(8):
+
+    def q_three(c):
+        two[c].wait_recv()
+        added(c, 2, r2)
+        three[c] = start(2, c, part.at[c, pl.ds(1, 1)], r3.at[c])
+
+    def q_end(c):
         three[c].wait_recv()
         total = part[c, 0].astype(F32) + r3[c, 0].astype(F32)
-        out[pl.ds(c * 128, 128), :] = total.T
+        out_q[pl.ds(c * 128, 128), :] = total.T
+
+    lagged = (
+        (q_two, 0), (out_high, -2), (q_three, 1), (out_low, 0),
+        (q_end, 2), (out_y, 1), (out_end, 2),
+    )
+    for n in range(-2, 8 + 3):
+        for action, lag in lagged:
+            j = n - lag
+            if action is out_high and j < 2:
+                continue
+            if n >= 0 and 0 <= j < 8:
+                action(j)
     for copy in copies:
         copy.wait_send()
 
 
-def query_grad(normed, cot_rows, factor):
+def grads(normed, cot_rows, partials, factor):
+    shape = jax.ShapeDtypeStruct
     return pl.pallas_call(
-        functools.partial(query_grad_kernel, factor),
-        out_shape=jax.ShapeDtypeStruct((1024, 256), F32),
-        in_specs=vmem_specs(2),
-        out_specs=pl.BlockSpec(memory_space=pltpu.VMEM),
+        functools.partial(grads_kernel, factor),
+        out_shape=(shape((1024, 256), F32), shape((256, 1024), F32)),
+        in_specs=vmem_specs(2) + any_specs(1),
+        out_specs=tuple(vmem_specs(2)),
         scratch_shapes=[
             pltpu.VMEM((8, 8, 256, 128), BF),
             pltpu.VMEM((8, 4, 256, 128), BF),
             pltpu.VMEM((8, 2, 256, 128), BF),
             pltpu.VMEM((8, 1, 256, 128), BF),
-            pltpu.SemaphoreType.DMA((24,)),
-            pltpu.SemaphoreType.DMA((24,)),
+            pltpu.VMEM((2, 4, 2, 256, 512), BF),
+            pltpu.VMEM((2, 4, 2, 256, 512), BF),
+            pltpu.VMEM((2, 2, 2, 256, 512), BF),
+            pltpu.VMEM((2, 2, 256, 512), BF),
+            pltpu.VMEM((2, 256, 512), BF),
+            pltpu.SemaphoreType.DMA((1,)),
+            pltpu.SemaphoreType.DMA((56,)),
+            pltpu.SemaphoreType.DMA((56,)),
         ],
         compiler_params=pltpu.CompilerParams(
             collective_id=1, has_side_effects=True, vmem_limit_bytes=VMEM_BYTES
         ),
-        name="query_grad",
-    )(normed, cot_rows)
-
-
-DP_PEERS = [(x, yh, 0, 0, 0) for x in range(4) for yh in range(2) if x or yh]
-TENSOR_PEERS = [(0, 0, z, yl, c) for z in range(4) for yl in range(2) for c in range(2) if z or yl or c]
+        name="grads",
+    )(normed, cot_rows, partials)
 
 
 def sum_over(here, slots_dp, slots_tensor, staged, sent, got, at):
@@ -570,14 +848,14 @@
     output_scale = qwidth ** (-0.5)
     gn_scale = qwidth / (row_count * groups)
     param_count = 2.0 * D * qwidth
-    dir_output = basis_output[K - 1]
-    query, tangent, key_states, values, normed, gram = project(
+    query, tangent, key_states, values, normed, gram, wall = project(
         tokens.reshape(row_count, model_width),
         norm_gain.reshape(1, model_width),
         q_weight,
         basis_query,
         kv_weight,
         basis_output,
+        o_weight,
     )
     allowed = allowed_pairs(segments)
     query_wide = query.astype(jnp.float32).reshape(seq_count, length, heads_dev, HD)
@@ -591,26 +869,14 @@
     heads_out, tangent_heads = jax.jvp(attend_here, (query_wide,), (tangent_wide,))
     heads_out = heads_out.reshape(row_count, col_count).astype(jnp.bfloat16)
     tangent_heads = tangent_heads.reshape(row_count, col_count).astype(jnp.bfloat16)
-    all_heads, all_tangent = sent_together((heads_out, tangent_heads), DP, 0, 1)
-    group_term = jnp.dot(
-        all_heads, dir_output, preferred_element_type=jnp.float32
-    ) * output_scale + jnp.dot(all_tangent, o_weight, preferred_element_type=jnp.float32)
-    tangent_columns = (
-        total_of(group_term.astype(jnp.bfloat16), TENSOR).astype(jnp.float32).astype(jnp.bfloat16)
-    )
-    cot_heads = lax.psum_scatter(
-        lax.dot_general(
-            tangent_columns, o_weight, (((1,), (1,)), ((), ())), preferred_element_type=jnp.float32
-        ).astype(jnp.bfloat16),
-        DP,
-        scatter_dimension=0,
-        tiled=True,
-    ).astype(jnp.float32)
-    gn_output = block_products(all_heads, tangent_columns, groups, gn_scale * output_scale)
+    heads_out = heads_out * jnp.bfloat16(output_scale)
+    both_heads = jnp.concatenate([heads_out, tangent_heads], axis=1)
+    cot_heads, partials = output_side(both_heads.reshape(16, 2, 16, 2 * col_count), wall)
+    cot_heads = cot_heads.astype(jnp.float32)
     _, pullback = jax.vjp(attend_here, query_wide)
     cot_query = pullback(cot_heads.reshape(seq_count, length, heads_dev, HD))[0]
     cot_query = cot_query.reshape(row_count, col_count).astype(jnp.bfloat16)
-    gn_query = query_grad(normed, cot_query.T, gn_scale * query_scale)
+    gn_query, gn_output = grads(normed, cot_query.T, partials, gn_scale * query_scale)
     next_query, next_output, lines = clean(
         gn_query, gn_output, basis_query, basis_output, gram, param_count
     )

time: 536 us -> 352 us (0.66)
  waiting for transfers between devices: 285 us -> 0 us
  Pallas kernels: 173 us -> 328 us
  matrix products: 39.5 us -> 6.73 us
  between operations: 14 us -> 0.85 us
    reduce_scatter x2 -> x0, waiting for transfers between devices: 160 us -> none  [the longest x1 94.6 us: total_of(): lax.psum_scatter(filled_up(lines, lax.axis_size(axis)), axis, scatter_dim...]
    all_gather x2 -> x0, waiting for transfers between devices: 126 us -> none  [the longest x1 71 us: sent_together(): lax.all_gather(both, axis, axis=dim, tiled=True)]
    pallas_call x1 -> x2, Pallas kernels: 41.5 us -> 145 us  [the longest x1 81.2 us: output_side(): pl.pallas_call(output_kernel, out_shape=(shape((16, 2, 16, 256), BF), sha...]
    pallas_call x1, Pallas kernels: 87.3 us -> 143 us  [project(): pl.pallas_call(project_kernel, out_shape=(shape((512, 256), BF), shape((5...]
    dot_general x4 -> x0, matrix products: 32.1 us -> none  [the longest x1 9.91 us: body(): jnp.dot(all_heads, dir_output, preferred_element_type=jnp.float32)]
  transfers between devices with their start and end apart: 4 -> 0, of which waited for: 4 -> 0; matrix products, arithmetic and copies ran while one was open for 1% -> 0% of each run, Pallas kernels for 0% -> 0%
where the time goes in v2:
time: 352 us
  Pallas kernels  328 us (93%)
  local copies, waits for them, and re-layouts  11.6 us (3%)
  matrix products  6.73 us (2%)
  other arithmetic  4.49 us (1%)
    pallas_call x1, Pallas kernels, project(): pl.pallas_call(project_kernel, out_shape=(shape((512, 256), BF), shape((5...  143 us
    pallas_call x1, Pallas kernels, output_side(): pl.pallas_call(output_kernel, out_shape=(shape((16, 2, 16, 256), BF), sha...  81.2 us
    pallas_call x1, Pallas kernels, grads(): pl.pallas_call(functools.partial(grads_kernel, factor), out_shape=(shape(...  64.1 us
    pallas_call x1, Pallas kernels, clean(): pl.pallas_call(functools.partial(clean_kernel, count), out_shape=(shape((...  39.7 us

profile of v2, /device:TPU:1, one launch (start us, length us, event | category | flops | bytes accessed | tf_op | source)
XLA Modules:
  0.0 351.6 jit_solution(10997877612383807112)
XLA Ops:
  0.7 1.0 compare_and_fusion.1
  1.7 0.3 copy.27
  2.0 0.5 fusion.38
  2.5 142.9 %project.1 = (bf16[512,256]{1,0:T(8,128)(2,1)}, bf16[512,256]{1,0:T(8,128)(2,1)}, bf16[512,128]{1,0:T(8,128)(2,1)}, bf16[512,128]{1,0:T(8,128)(2,1)}, bf16[512,8...) custom-call(bf16[512,8192]{1,0:T(8,128)(2,1)} %bitcast.87, f32[1,8192]{1,0:T(1,128)} %bitcast.95, ...), custom_call_target="tpu_custom_call" | custom-call | tf_op jit(solution)/shard_map/project/pallas_call | solution.py:357
  145.4 0.9 convert.3
  146.3 0.2 multiply_subtract_fusion.2
  146.5 1.2 reshape.179
  147.7 1.2 reshape.181
  148.9 0.0 copy-start
  148.9 1.1 fusion.47
  150.0 0.3 multiply_subtract_fusion.1
  150.4 1.2 fusion.17
  151.6 0.2 fusion.39
  151.8 1.4 fusion.49
  153.2 0.0 copy-done
  153.3 0.8 fusion.3
  154.1 0.2 copy.37
  154.3 0.2 convert_element_type.30
  154.5 0.7 fusion.5
  155.2 0.2 copy.32
  155.4 0.2 mul.415
  155.5 0.9 pad_maximum_fusion.h
  156.4 81.2 %output_side.1 = (bf16[16,2,16,256]{3,2,1,0:T(8,128)(2,1)}, bf16[2,2,4,2,256,512]{5,4,3,2,1,0:T(8,128)(2,1)}) custom-call(bf16[16,2,16,512]{3,2,1,0:T(8,128)(2,1)} %pad_maximum_fusion.h, bf16[2,16,256,1024]{3,2,1,0:T(8,128)(2,1)} %get-tuple-element.22.wall), custom_call_target="tpu_custom_call" | custom-call | tf_op jit(solution)/shard_map/output_side/pallas_call | solution.py:542
  237.6 1.0 reshape.175
  238.6 0.1 copy.38
  238.8 0.4 multiply_reduce_fusion
  239.2 2.1 fusion.15
  241.3 0.2 multiply_add_fusion.1
  241.6 0.2 add_convert_fusion
  241.8 0.2 copy.42
  242.0 0.7 copy.61
  242.7 64.1 %grads.1 = (f32[1024,256]{1,0:T(8,128)}, f32[256,1024]{1,0:T(8,128)}) custom-call(bf16[512,8192]{1,0:T(8,128)(2,1)} %get-tuple-element.17.normed, bf16[256,512]{1,0:T(8,128)(2,1)} %bitcast.88, bf16[2,2,4,2,256,512]{5,4,3,2,1,0:T(8,128)(2,1)} %get-tuple-element.24.gp), custom_call_target="tpu_custom_call" | custom-call | tf_op jit(solution)/shard_map/grads/pallas_call | solution.py:696
  306.9 39.7 %clean.1 = (bf16[1024,256]{1,0:T(8,128)(2,1)}, bf16[256,1024]{1,0:T(8,128)(2,1)}, f32[16,128]{1,0:T(8,128)}) custom-call(f32[1024,256]{1,0:T(8,128)} %get-tuple-element.25.gq, f32[256,1024]{1,0:T(8,128)} %get-tuple-element.26.go, bf16[8,1024,256]{2,1,0:T(8,128)(2,1)} %vq.1, bf16[8,256,1024]{2,1,0:T(8,128)(2,1)} %vo.1, f32[64,128]{1,0:T(8,128)} %get-tuple-element.27.gram), custom_call_target="tpu_custom_call" | custom-call | tf_op jit(solution)/shard_map/clean/pallas_call | solution.py:817
  346.6 1.3 slice_reduce_fusion
  347.9 1.9 copy.72
  349.8 1.9 copy.73
  (5 shorter events, 0.1 us)
Async XLA Ops:
  148.9 4.4 %copy-start = (bf16[512,128]{1,0:T(8,128)(2,1)S(1)}, bf16[512,128]{1,0:T(8,128)(2,1)}, u32[]{:S(2)}) copy-start(bf16[512,128]{1,0:T(8,128)(2,1)} %get-tuple-element.18) | copy-start | bytes 393220

commit v3 on v2

v3 whole, which is shorter than its diff:
```python
import functools
import math

import jax
import jax.numpy as jnp
from jax import lax
from jax.experimental import pallas as pl
from jax.experimental.pallas import tpu as pltpu
from jax.sharding import Mesh
from jax.sharding import PartitionSpec as P

D = 8192
HD = 128
QH = 32
KVH = 4
K = 8
DP = ("dp_0", "dp_1")
TENSOR = ("tensor_0", "tensor_1", "tensor_2")
DP_TENSOR = ("dp_0", "dp_1", "tensor_0", "tensor_1", "tensor_2")


PRECISE = lax.Precision.HIGHEST
ROPE_BASE = 500000.0
NORM_EPS = 1e-05
BETA_EPS = 1e-06


MESH = pl.DeviceIdType.MESH
VMEM_BYTES = 58 * 1024 * 1024
X1, X3, X2, YH = (1, 0, 0, 0, 0), (3, 0, 0, 0, 0), (2, 0, 0, 0, 0), (0, 1, 0, 0, 0)
Z1, Z3, YL, CORE = (0, 0, 1, 0, 0), (0, 0, 3, 0, 0), (0, 0, 0, 1, 0), (0, 0, 0, 0, 1)
BF = jnp.bfloat16
F32 = jnp.float32


def position():
    return [lax.axis_index(a) for a in DP_TENSOR]


def flipped(value, mask):
    if mask == 0:
        return value
    if mask == 1:
        return value + 1 - 2 * lax.rem(value, 2)
    if mask == 2:
        return lax.rem(value + 2, 4)
    return 3 - value


def peer(here, masks):
    return tuple(flipped(v, m) for v, m in zip(here, masks))


def greet(here, peers):
    barrier = pltpu.get_barrier_semaphore()
    for masks in peers:
        pl.semaphore_signal(barrier, inc=1, device_id=peer(here, masks), device_id_type=MESH)
    pl.semaphore_wait(barrier, len(peers))


def send(src, dst, send_sem, recv_sem, here, masks):
    copy = pltpu.make_async_remote_copy(
        src_ref=src,
        dst_ref=dst,
        send_sem=send_sem,
        recv_sem=recv_sem,
        device_id=peer(here, masks),
        device_id_type=MESH,
    )
    copy.start()
    return copy


def dp_source(here, bits, stages):
    x, yh = here[0], here[1]
    for bit, masks in zip(bits, stages):
        if masks[0] == 1:
            x = x + bit * (1 - 2 * lax.rem(x, 2))
        elif masks[0] == 3:
            x = x + bit * (3 - 2 * x)
        else:
            yh = yh + bit * (1 - 2 * yh)
    return x * 2 + yh


STAGES = ((X1, YH, X3), (X3, YH, X1))
IN_STAGES = ((X1, YH, X3), (X3, YH, X1), (X1, YH, X3), (X3, YH, X1))
OUT_STAGES = ((YL, Z1, Z3), (YL, Z3, Z1))


DP_PEERS = [(x, yh, 0, 0, 0) for x in range(4) for yh in range(2) if x or yh]
TENSOR_PEERS = [(0, 0, z, yl, c) for z in range(4) for yl in range(2) for c in range(2) if z or yl or c]


def z_place(mask, kind):
    one, three = {0: (0, 0), 1: (1, 0), 3: (0, 1), 2: (1, 1)}[mask]
    return one + 2 * three if kind == 0 else three + 2 * one


def out_place(r, kind):
    mz, ml = r // 2, r % 2
    return ml + 2 * z_place(mz, kind)


def same_core_masks(r):
    return (0, 0, r // 2, r % 2, 0)


def rope_tables(length, head_width):
    half_width = head_width // 2
    frequency = jnp.exp(
        jnp.arange(half_width, dtype=jnp.float32) * (-2.0 * math.log(ROPE_BASE) / head_width)
    )
    angles = jnp.arange(length, dtype=jnp.float32)[:, None] * frequency[None, :]
    return (jnp.cos(angles), jnp.sin(angles))


def rotate(vectors, cosine_table, sine_table):
    half_width = vectors.shape[-1] // 2
    front_half = vectors[..., :half_width]
    back_half = vectors[..., half_width:]
    return jnp.concatenate(
        [
            front_half * cosine_table - back_half * sine_table,
            front_half * sine_table + back_half * cosine_table,
        ],
        axis=-1,
    )


def attend(query, key_states, values, allowed):
    length = query.shape[1]
    head_width = query.shape[-1]
    cosine_table, sine_table = rope_tables(length, head_width)
    query = rotate(query, cosine_table[:, None, :], sine_table[:, None, :])
    key_states = rotate(key_states, cosine_table, sine_table)
    scores = jnp.einsum("slgd,smd->sglm", query, key_states, precision=PRECISE) * head_width ** (
        -0.5
    )
    scores = jnp.where(allowed[:, None, :, :], scores, -1e30)
    row_max = lax.stop_gradient(jnp.max(scores, axis=-1, keepdims=True))
    weights = jnp.exp(scores - row_max)
    probabilities = weights / jnp.sum(weights, axis=-1, keepdims=True)
    return jnp.einsum("sglm,smd->slgd", probabilities, values, precision=PRECISE)


def allowed_pairs(segments):
    length = segments.shape[1]
    position = jnp.arange(length, dtype=jnp.int32)
    causal = position[:, None] >= position[None, :]
    return jnp.logical_and(segments[:, :, None] == segments[:, None, :], causal[None])


SUPER = (0, 1) * 4 + (2, 3) * 4
PIECE = (0, 0, 1, 1, 2, 2, 3, 3) * 2


def project_kernel(
    count, tok, gain, q_w, vec_q, kv_w, vec_o, o_w,
    q_out, t_out, k_out, v_out, normed_out, gram_out, wall,
    x, buf, acc, mine, theirs, vq, vo, w, g1, g2, load, sent, got,
):
    here = position()
    core = here[4]
    kv_head = here[2]
    for_rows = []
    for s in range(4):
        rows = pl.ds(s * 256, 256)
        kv_cols = pl.ds(pl.multiple_of(kv_head * HD, HD), HD)
        parts = (
            (q_w.at[rows], buf.at[s, 0, :, pl.ds(0, 256)]),
            (vec_q.at[K - 1, rows], buf.at[s, 0, :, pl.ds(256, 256)]),
            (kv_w.at[core, rows, kv_cols], buf.at[s, 0, :, pl.ds(512, 128)]),
        )
        for n, (src, dst) in enumerate(parts):
            copy = pltpu.make_async_copy(src, dst, load.at[3 * s + n])
            copy.start()
            for_rows.append(copy)
    own_out = []
    for kind, src in enumerate((vec_o.at[K - 1], o_w)):
        copy = pltpu.make_async_copy(src, w.at[kind, 0], load.at[16 + kind])
        copy.start()
        own_out.append(copy)
    greet(here, DP_PEERS + TENSOR_PEERS)
    for copy in for_rows:
        copy.wait()

    def start_stage(stage, k):
        s, rows = SUPER[k], pl.ds(PIECE[k] * 64, 64)
        n = 1 << stage
        at = stage * 16 + k
        return send(
            buf.at[s, pl.ds(0, n), rows],
            buf.at[s, pl.ds(n, n), rows],
            sent.at[at],
            got.at[at],
            here,
            IN_STAGES[s][stage],
        )

    out_copies = {}

    def start_out(stage, kind, piece):
        n = 1 << stage
        rows = pl.ds(piece * 64, 64)
        at = 49 + stage * 8 + kind * 4 + piece
        out_copies[stage, kind, piece] = send(
            w.at[kind, pl.ds(0, n), rows],
            w.at[kind, pl.ds(n, n), rows],
            sent.at[at],
            got.at[at],
            here,
            OUT_STAGES[kind][stage],
        )

    def next_out(stage, piece):
        for kind in range(2):
            out_copies[stage, kind, piece].wait_recv()
            start_out(stage + 1, kind, piece)

    for copy in own_out:
        copy.wait()
    for kind in range(2):
        start_out(0, kind, 0)
    first = [start_stage(0, k) for k in range(16)]
    tok_copy = pltpu.make_async_copy(tok, x, load.at[12])
    tok_copy.start()
    vq_copy = pltpu.make_async_copy(vec_q, vq, load.at[13])
    vq_copy.start()
    vo_copy = pltpu.make_async_copy(vec_o, vo, load.at[14])
    vo_copy.start()
    wall_copies = []

    def keep_wall(kind, lo):
        copy = pltpu.make_async_copy(
            w.at[kind, pl.ds(lo, 4)], wall.at[kind, pl.ds(lo, 4)], load.at[18 + kind + lo // 2]
        )
        copy.start()
        wall_copies.append(copy)

    dp = here[0] * 2 + here[1]
    tensor = here[2] * 4 + here[3] * 2 + here[4]

    def exchange(slots, own, peers, base):
        ref = slots.at[own]
        return [
            send(ref, ref, sent.at[base + n], got.at[base + n], here, masks)
            for n, masks in enumerate(peers)
        ]

    def norm_rows(lo, hi):
        def step(i, carry):
            rows = pl.ds(pl.multiple_of(i * 16, 16), 16)
            total = jnp.zeros((16, 1), F32)
            for c in range(8):
                part = x[rows, pl.ds(c * 1024, 1024)].astype(F32)
                total += jnp.sum(part * part, axis=1, keepdims=True)
            inv = lax.rsqrt(total / D + NORM_EPS)
            for c in range(8):
                cols = pl.ds(c * 1024, 1024)
                x[rows, cols] = (x[rows, cols].astype(F32) * inv * gain[:, cols]).astype(BF)
            return carry

        lax.fori_loop(lo // 16, hi // 16, step, 0)

    def dots(s, lo, hi):
        def step(p, carry):
            bits = (lax.rem(p, 2), lax.rem(p // 2, 2), p // 4)
            source = dp_source(here, bits, IN_STAGES[s])
            cols = pl.ds(pl.multiple_of(source * 1024 + s * 256, 256), 256)
            acc[...] += jnp.dot(x[:, cols], buf[s, p], preferred_element_type=F32)
            return carry

        lax.fori_loop(lo, hi, step, 0)

    def gram():
        pairs = [(i, j) for i in range(K) for j in range(i, K)]

        def tile(ref, rows, cols, carry):
            b = [ref[j, rows, cols].astype(F32) for j in range(K)]
            out = []
            for (i, j), a in zip(pairs, carry):
                p = b[i] * b[j]
                out.append(a + (p[:8] + p[8:]))
            return tuple(out)

        def step_q(r, carry):
            rows = pl.ds(pl.multiple_of(r * 16, 16), 16)
            for h in range(2):
                carry = tile(vq, rows, pl.ds(h * 128, 128), carry)
            return carry

        def step_o(r, carry):
            rows = pl.ds(pl.multiple_of(r * 16, 16), 16)
            for h in range(8):
                carry = tile(vo, rows, pl.ds(h * 128, 128), carry)
            return carry

        carry = tuple(jnp.zeros((8, 128), F32) for _ in pairs)
        carry = lax.fori_loop(0, 64, step_q, carry)
        carry = lax.fori_loop(0, 16, step_o, carry)
        lane = lax.broadcasted_iota(jnp.int32, (8, 128), 1)
        row = lax.broadcasted_iota(jnp.int32, (8, 128), 0)
        tile_sum = jnp.zeros((8, 128), F32)
        for (i, j), a in zip(pairs, carry):
            value = jnp.sum(jnp.sum(a, axis=0, keepdims=True), axis=1, keepdims=True)
            hit = jnp.logical_or(
                jnp.logical_and(lane == i, row == j), jnp.logical_and(lane == j, row == i)
            )
            tile_sum = tile_sum + jnp.where(hit, value, 0.0)
        g1[dp] = tile_sum

    acc[...] = jnp.zeros_like(acc)
    second, third = [], []
    out_steps = {
        1: (0, 0), 2: (0, 1), 4: (0, 2), 6: (0, 3), 3: (1, 0), 5: (1, 1), 7: (1, 2), 9: (1, 3)
    }
    for k in range(16):
        first[k].wait_recv()
        second.append(start_stage(1, k))
        if k >= 1:
            second[k - 1].wait_recv()
            third.append(start_stage(2, k - 1))
        if k in out_steps:
            stage, piece = out_steps[k]
            next_out(stage, piece)
        if k in (0, 2, 4):
            start_out(0, 0, k // 2 + 1)
            start_out(0, 1, k // 2 + 1)
        if k == 0:
            tok_copy.wait()
            norm_rows(0, 256)
        if k == 1:
            norm_rows(256, 512)
            out_copy = pltpu.make_async_copy(x, normed_out, load.at[15])
            out_copy.start()
        if k == 2:
            vq_copy.wait()
            vo_copy.wait()
            gram()
            over_dp = exchange(g1, dp, DP_PEERS, 73)
        if k == 8:
            dots(0, 0, 4)
        if k == 9:
            dots(1, 0, 4)
        if k == 10:
            keep_wall(0, 0)
            keep_wall(1, 0)
            for copy in over_dp:
                copy.wait_recv()
            total = g1[0]
            for n in range(1, 8):
                total = total + g1[n]
            g2[tensor] = total
            over_tensor = exchange(g2, tensor, TENSOR_PEERS, 80)
        if k == 13:
            for n in (0, 2, 4, 6):
                third[n].wait_recv()
            dots(0, 4, 8)
        if k == 14:
            for n in (1, 3, 5, 7):
                third[n].wait_recv()
            dots(1, 4, 8)
        if k == 15:
            dots(2, 0, 4)
    second[15].wait_recv()
    third.append(start_stage(2, 15))
    dots(3, 0, 4)
    for s in (2, 3):
        for n in range(8, 16):
            if SUPER[n] == s:
                third[n].wait_recv()
        dots(s, 4, 8)
    mine[...] = acc[:, pl.ds(512, 128)].astype(BF)
    swap = send(mine, theirs, sent.at[48], got.at[48], here, CORE)
    q_out[...] = acc[:, pl.ds(0, 256)].astype(BF)
    t_out[...] = (acc[:, pl.ds(256, 256)] * (D ** (-0.5))).astype(BF)
    swap.wait()
    own = mine[...].astype(F32)
    other = theirs[...].astype(F32)
    first_core = core == 0
    k_out[...] = jnp.where(first_core, own, other).astype(BF)
    v_out[...] = jnp.where(first_core, other, own).astype(BF)
    for kind in range(2):
        for piece in range(4):
            out_copies[2, kind, piece].wait_recv()
        keep_wall(kind, 4)
    for copy in over_tensor:
        copy.wait_recv()
    total = g2[0]
    for n in range(1, 16):
        total = total + g2[n]
    gram_out[...] = total / count
    for copy in first + second + third + list(out_copies.values()) + over_dp + over_tensor:
        copy.wait_send()
    for copy in wall_copies:
        copy.wait()
    out_copy.wait()


def any_specs(n):
    return [pl.BlockSpec(memory_space=pl.ANY) for _ in range(n)]


def vmem_specs(n):
    return [pl.BlockSpec(memory_space=pltpu.VMEM) for _ in range(n)]


def project(tokens, norm_gain, q_weight, basis_query, kv_weight, basis_output, o_weight, count):
    shape = jax.ShapeDtypeStruct
    return pl.pallas_call(
        functools.partial(project_kernel, count),
        out_shape=(
            shape((512, 256), BF),
            shape((512, 256), BF),
            shape((512, HD), BF),
            shape((512, HD), BF),
            shape((512, D), BF),
            shape((8, 128), F32),
            shape((2, 8, 256, 1024), BF),
        ),
        in_specs=any_specs(1) + vmem_specs(1) + any_specs(5),
        out_specs=tuple(vmem_specs(4) + any_specs(1) + vmem_specs(1) + any_specs(1)),
        scratch_shapes=[
            pltpu.VMEM((512, D), BF),
            pltpu.VMEM((4, 8, 256, 640), BF),
            pltpu.VMEM((512, 640), F32),
            pltpu.VMEM((512, HD), BF),
            pltpu.VMEM((512, HD), BF),
            pltpu.VMEM((K, 1024, 256), BF),
            pltpu.VMEM((K, 256, 1024), BF),
            pltpu.VMEM((2, 8, 256, 1024), BF),
            pltpu.VMEM((8, 8, 128), F32),
            pltpu.VMEM((16, 8, 128), F32),
            pltpu.SemaphoreType.DMA((22,)),
            pltpu.SemaphoreType.DMA((95,)),
            pltpu.SemaphoreType.DMA((95,)),
        ],
        compiler_params=pltpu.CompilerParams(
            collective_id=0, has_side_effects=True, vmem_limit_bytes=VMEM_BYTES
        ),
        name="project",
    )(tokens, norm_gain, q_weight, basis_query, kv_weight, basis_output, o_weight)


def output_kernel(
    h, wall, cot, gp_out,
    w, g, acc, tb, mine, theirs, cs, c1, c2, c3, gp, load, sent, got,
):
    here = position()
    place = here[2] * 2 + here[3]
    loads = []
    for kind in (0, 1):
        copy = pltpu.make_async_copy(wall.at[kind], w.at[kind], load.at[kind])
        copy.start()
        loads.append(copy)
    greet(here, [X1, X3, YH, CORE] + [same_core_masks(r) for r in range(1, 8)])
    copies = []

    def start(at, src, dst, masks):
        copy = send(src, dst, sent.at[at], got.at[at], here, masks)
        copies.append(copy)
        return copy

    def index_of(r):
        z, yl = peer(here[2:4], same_core_masks(r)[2:4])
        return z * 2 + yl

    spread = {
        r: start(r, h.at[index_of(r)], g.at[:, r, 0], same_core_masks(r)) for r in range(1, 8)
    }
    g[:, 0, 0] = h[place]

    def gather(stage, rg, kind):
        n = 1 << stage
        group = pl.ds(rg * 2, 2)
        return start(
            8 + stage * 8 + rg * 2 + kind,
            g.at[kind, group, pl.ds(0, n)],
            g.at[kind, group, pl.ds(n, n)],
            STAGES[kind][stage],
        )

    one, two, three = {}, {}, {}
    for rg in range(4):
        for r in (rg * 2, rg * 2 + 1):
            if r:
                spread[r].wait_recv()
        for kind in range(2):
            one[rg, kind] = gather(0, rg, kind)
    order = [(rg, kind) for rg in range(4) for kind in range(2)]
    for n, key in enumerate(order):
        one[key].wait_recv()
        two[key] = gather(1, *key)
        if n >= 1:
            two[order[n - 1]].wait_recv()
            three[order[n - 1]] = gather(2, *order[n - 1])
    two[order[7]].wait_recv()
    three[order[7]] = gather(2, *order[7])

    def rows_of(r, cols):
        parts = [g[kind, r, :, :, cols].reshape(256, 256) for kind in range(2)]
        return jnp.concatenate(parts, axis=0)

    for copy in loads:
        copy.wait()
    acc[...] = jnp.zeros_like(acc)
    for rg in range(4):
        three[rg, 0].wait_recv()
        three[rg, 1].wait_recv()
        for r in (rg * 2, rg * 2 + 1):
            acc[...] += jnp.dot(
                rows_of(r, pl.ds(0, 256)), w[0, out_place(r, 0)], preferred_element_type=F32
            ) + jnp.dot(
                rows_of(r, pl.ds(256, 256)), w[1, out_place(r, 1)], preferred_element_type=F32
            )
    swaps = []
    for half in range(2):
        rows = pl.ds(half * 256, 256)
        mine[rows] = acc[rows].astype(BF)
        swaps.append(start(56 + half, mine.at[rows], theirs.at[rows], CORE))
    for half in range(2):
        rows = pl.ds(half * 256, 256)
        swaps[half].wait_recv()
        tb[rows] = (mine[rows].astype(F32) + theirs[rows].astype(F32)).astype(BF)

    def scatter(stage, key, src, dst):
        rg, kind = key
        return start(32 + stage * 8 + rg * 2 + kind, src, dst, STAGES[kind][2 - stage])

    one, two, three = {}, {}, {}
    for rg in range(4):
        group = pl.ds(rg * 2, 2)
        for r in (rg * 2, rg * 2 + 1):
            part = lax.dot_general(
                tb[...],
                w[1, out_place(r, 1)],
                (((1,), (1,)), ((), ())),
                preferred_element_type=F32,
            ).astype(BF)
            for kind in range(2):
                cs[kind, r] = part[kind * 256 : kind * 256 + 256].reshape(8, 32, 256)
        for kind in range(2):
            one[rg, kind] = scatter(
                0, (rg, kind), cs.at[kind, group, pl.ds(4, 4)], c1.at[kind, group]
            )

    def added(key, n, ref):
        rg, kind = key
        group = pl.ds(rg * 2, 2)
        cs[kind, group, pl.ds(0, n)] = (
            cs[kind, group, pl.ds(0, n)].astype(F32) + ref[kind, group].astype(F32)
        ).astype(BF)

    def output_grad(r):
        mz, ml = r // 2, r % 2
        block = lax.dot_general(
            rows_of(r, pl.ds(0, 256)),
            tb[...],
            (((0,), (0,)), ((), ())),
            preferred_element_type=F32,
        ).astype(BF)
        for kind in range(2):
            gp[kind, z_place(mz, kind), ml] = block[:, kind * 512 : kind * 512 + 512]

    def second(key):
        rg, kind = key
        one[key].wait_recv()
        added(key, 4, c1)
        group = pl.ds(rg * 2, 2)
        two[key] = scatter(1, key, cs.at[kind, group, pl.ds(2, 2)], c2.at[kind, group])

    def third(key):
        rg, kind = key
        two[key].wait_recv()
        added(key, 2, c2)
        group = pl.ds(rg * 2, 2)
        three[key] = scatter(2, key, cs.at[kind, group, pl.ds(1, 1)], c3.at[kind, group])

    for n, key in enumerate(order):
        second(key)
        if n >= 1:
            third(order[n - 1])
        output_grad(n)
    third(order[7])
    back = {}
    for rg in range(4):
        for kind in range(2):
            three[rg, kind].wait_recv()
            added((rg, kind), 1, c3)
        for r in (rg * 2, rg * 2 + 1):
            if r:
                back[r] = start(r + 58, cs.at[:, r, 0], cot.at[place], same_core_masks(r))
    cot[place] = cs[:, 0, 0]
    gp_copy = pltpu.make_async_copy(gp, gp_out, load.at[2])
    gp_copy.start()
    for r in range(1, 8):
        back[r].wait_recv()
    for copy in copies:
        copy.wait_send()
    gp_copy.wait()


def output_side(heads, wall):
    shape = jax.ShapeDtypeStruct
    return pl.pallas_call(
        output_kernel,
        out_shape=(shape((8, 2, 32, 256), BF), shape((2, 4, 2, 256, 512), BF)),
        in_specs=vmem_specs(1) + any_specs(1),
        out_specs=tuple(vmem_specs(1) + any_specs(1)),
        scratch_shapes=[
            pltpu.VMEM((2, 8, 256, 1024), BF),
            pltpu.VMEM((2, 8, 8, 32, 512), BF),
            pltpu.VMEM((512, 1024), F32),
            pltpu.VMEM((512, 1024), BF),
            pltpu.VMEM((512, 1024), BF),
            pltpu.VMEM((512, 1024), BF),
            pltpu.VMEM((2, 8, 8, 32, 256), BF),
            pltpu.VMEM((2, 8, 4, 32, 256), BF),
            pltpu.VMEM((2, 8, 2, 32, 256), BF),
            pltpu.VMEM((2, 8, 1, 32, 256), BF),
            pltpu.VMEM((2, 4, 2, 256, 512), BF),
            pltpu.SemaphoreType.DMA((3,)),
            pltpu.SemaphoreType.DMA((66,)),
            pltpu.SemaphoreType.DMA((66,)),
        ],
        compiler_params=pltpu.CompilerParams(
            collective_id=3, has_side_effects=True, vmem_limit_bytes=VMEM_BYTES
        ),
        name="output_side",
    )(heads, wall)


def tail_kernel(
    factor, count, normed_hbm, cot, gp, gram, vec_q, vec_o, clean_q, clean_o, coeffs,
    normed, part, r1, r2, r3, own, z1, z2, y1, vq, vo, gq, go, facc,
    s1, s2, u1, u2, load, sent, got,
):
    here = position()
    dp = here[0] * 2 + here[1]
    tensor = here[2] * 4 + here[3] * 2 + here[4]
    loads = []

    def fetch(src, dst):
        copy = pltpu.make_async_copy(src, dst, load.at[len(loads)])
        copy.start()
        loads.append(copy)

    fetch(gp, own)
    fetch(normed_hbm, normed)
    greet(here, DP_PEERS + TENSOR_PEERS)
    copies = []

    def keep(copy):
        copies.append(copy)
        return copy

    def rows_at(j):
        return pl.ds(j // 2 * 64, 64)

    def start_out(stage, j, src, dst):
        at = 24 + stage * 8 + j
        masks = ((Z3, Z1)[j % 2], (Z1, Z3)[j % 2], YL)[stage]
        return keep(send(src, dst, sent.at[at], got.at[at], here, masks))

    z_high, z_low, over_y = {}, {}, {}

    def out_high(j):
        kind, rows = j % 2, rows_at(j)
        z_high[j] = start_out(0, j, own.at[kind, pl.ds(2, 2), :, rows], z1.at[kind, :, :, rows])

    def out_low(j):
        kind, rows = j % 2, rows_at(j)
        z_high[j].wait_recv()
        own[kind, pl.ds(0, 2), :, rows] = (
            own[kind, pl.ds(0, 2), :, rows].astype(F32) + z1[kind, :, :, rows].astype(F32)
        ).astype(BF)
        z_low[j] = start_out(1, j, own.at[kind, 1, :, rows], z2.at[kind, :, rows])

    def out_y(j):
        kind, rows = j % 2, rows_at(j)
        z_low[j].wait_recv()
        own[kind, 0, :, rows] = (
            own[kind, 0, :, rows].astype(F32) + z2[kind, :, rows].astype(F32)
        ).astype(BF)
        over_y[j] = start_out(2, j, own.at[kind, 0, 1, rows], y1.at[kind, rows])

    def against(g, v, row0, tiles, col0, col_tiles):
        def step(i, state):
            rows = pl.ds(pl.multiple_of(row0 + i * 16, 16), 16)
            for h in range(col_tiles):
                cols = pl.ds(col0 + h * 128, 128)
                here_g = g[rows, cols]
                out = []
                for j in range(K):
                    p = here_g * v[j, rows, cols].astype(F32)
                    out.append(state[j] + (p[:8] + p[8:]))
                state = tuple(out)
            return state

        state = lax.fori_loop(0, tiles, step, tuple(facc[j] for j in range(K)))
        for j in range(K):
            facc[j] = state[j]

    def out_end(j):
        kind, rows = j % 2, rows_at(j)
        over_y[j].wait_recv()
        go[rows, pl.ds(kind * 512, 512)] = own[kind, 0, 0, rows].astype(F32) + y1[
            kind, rows
        ].astype(F32)
        against(go, vo, j // 2 * 64, 4, kind * 512, 4)

    def product(low, mid, high):
        source = dp_source(here, (low, mid, high), STAGES[0])
        cols = pl.ds(pl.multiple_of(source * 1024, 1024), 1024)
        block = jnp.dot(cot[...], normed[:, cols], preferred_element_type=F32) * factor
        block = block.astype(BF)
        for c in range(8):
            place = low + 2 * mid + 4 * high if c % 2 == 0 else high + 2 * mid + 4 * low
            part[c, place] = block[:, c * 128 : (c + 1) * 128]

    def start(stage, c, src, dst):
        at = stage * 8 + c
        return keep(send(src, dst, sent.at[at], got.at[at], here, STAGES[c % 2][2 - stage]))

    one, two, three = {}, {}, {}

    def q_one(c):
        one[c] = start(0, c, part.at[c, pl.ds(4, 4)], r1.at[c])

    loads[0].wait()
    for j in range(8):
        out_high(j)
    loads[1].wait()
    fetch(vec_q, vq)
    fetch(vec_o, vo)
    product(1, 0, 1)
    product(1, 1, 1)
    product(0, 0, 1)
    product(0, 1, 1)
    for c in (0, 2, 4, 6):
        q_one(c)
    product(1, 0, 0)
    product(1, 1, 0)
    for c in (1, 3, 5, 7):
        q_one(c)
    product(0, 0, 0)
    product(0, 1, 0)
    facc[...] = jnp.zeros_like(facc)

    def added(c, n, ref):
        part[c, pl.ds(0, n)] = (
            part[c, pl.ds(0, n)].astype(F32) + ref[c].astype(F32)
        ).astype(BF)

    def q_two(c):
        one[c].wait_recv()
        added(c, 4, r1)
        two[c] = start(1, c, part.at[c, pl.ds(2, 2)], r2.at[c])

    def q_three(c):
        two[c].wait_recv()
        added(c, 2, r2)
        three[c] = start(2, c, part.at[c, pl.ds(1, 1)], r3.at[c])

    def q_end(c):
        three[c].wait_recv()
        total = part[c, 0].astype(F32) + r3[c, 0].astype(F32)
        gq[pl.ds(c * 128, 128), :] = total.T
        against(gq, vq, c * 128, 8, 0, 2)

    lagged = ((q_two, 0), (out_low, 0), (q_three, 1), (out_y, 1), (q_end, 2), (out_end, 2))
    for n in range(8 + 2):
        if n == 2:
            loads[2].wait()
            loads[3].wait()
        for action, lag in lagged:
            if 0 <= n - lag < 8:
                action(n - lag)

    def exchange(slots, own_slot, peers, base):
        ref = slots.at[own_slot]
        return [
            keep(send(ref, ref, sent.at[base + n], got.at[base + n], here, masks))
            for n, masks in enumerate(peers)
        ]

    def sum_over(over_dp, over_tensor, base):
        for copy in exchange(over_dp, dp, DP_PEERS, base):
            copy.wait_recv()
        total = over_dp[0]
        for n in range(1, 8):
            total = total + over_dp[n]
        over_tensor[tensor] = total
        for copy in exchange(over_tensor, tensor, TENSOR_PEERS, base + 7):
            copy.wait_recv()
        total = over_tensor[0]
        for n in range(1, 16):
            total = total + over_tensor[n]
        return total

    for j in range(K):
        s1[dp, pl.ds(j, 1)] = jnp.sum(facc[j], axis=0, keepdims=True)
    first = jnp.sum(sum_over(s1, s2, 48), axis=1, keepdims=True) / count
    second = first
    for i in range(K):
        second = second - gram[:, pl.ds(i, 1)] * first[i : i + 1]
    both = first + second
    weights = [jnp.broadcast_to(both[j : j + 1], (16, 128)) for j in range(K)]

    def cleaned(g, v, c, row_tiles, col_tiles, state):
        def step(r, state):
            rows = pl.ds(pl.multiple_of(r * 16, 16), 16)
            for h in range(col_tiles):
                cols = pl.ds(h * 128, 128)
                value = g[rows, cols]
                for j in range(K):
                    value = value - weights[j] * v[j, rows, cols].astype(F32)
                c[rows, cols] = value
                p = value * value
                state = state + (p[:8] + p[8:])
            return state

        return lax.fori_loop(0, row_tiles, step, state)

    state = cleaned(gq, vq, clean_q, 64, 2, jnp.zeros((8, 128), F32))
    u1[dp] = cleaned(go, vo, clean_o, 16, 8, state)
    squares = sum_over(u1, u2, 70)
    squares = jnp.sum(jnp.sum(squares, axis=1, keepdims=True), axis=0, keepdims=True) / count
    beta = jnp.sqrt(squares + BETA_EPS)
    coeffs[pl.ds(0, 8)] = jnp.broadcast_to(both, (8, 128))
    coeffs[pl.ds(8, 8)] = jnp.broadcast_to(beta, (8, 128))
    for copy in copies:
        copy.wait_send()


def tail(normed, cot_rows, partials, gram, basis_query, basis_output, factor, count):
    shape = jax.ShapeDtypeStruct
    return pl.pallas_call(
        functools.partial(tail_kernel, factor, count),
        out_shape=(shape((1024, 256), F32), shape((256, 1024), F32), shape((16, 128), F32)),
        in_specs=any_specs(1) + vmem_specs(1) + any_specs(1) + vmem_specs(1) + any_specs(2),
        out_specs=tuple(vmem_specs(3)),
        scratch_shapes=[
            pltpu.VMEM((512, D), BF),
            pltpu.VMEM((8, 8, 256, 128), BF),
            pltpu.VMEM((8, 4, 256, 128), BF),
            pltpu.VMEM((8, 2, 256, 128), BF),
            pltpu.VMEM((8, 1, 256, 128), BF),
            pltpu.VMEM((2, 4, 2, 256, 512), BF),
            pltpu.VMEM((2, 2, 2, 256, 512), BF),
            pltpu.VMEM((2, 2, 256, 512), BF),
            pltpu.VMEM((2, 256, 512), BF),
            pltpu.VMEM((K, 1024, 256), BF),
            pltpu.VMEM((K, 256, 1024), BF),
            pltpu.VMEM((1024, 256), F32),
            pltpu.VMEM((256, 1024), F32),
            pltpu.VMEM((K, 8, 128), F32),
            pltpu.VMEM((8, 8, 128), F32),
            pltpu.VMEM((16, 8, 128), F32),
            pltpu.VMEM((8, 8, 128), F32),
            pltpu.VMEM((16, 8, 128), F32),
            pltpu.SemaphoreType.DMA((4,)),
            pltpu.SemaphoreType.DMA((92,)),
            pltpu.SemaphoreType.DMA((92,)),
        ],
        compiler_params=pltpu.CompilerParams(
            collective_id=1, has_side_effects=True, vmem_limit_bytes=VMEM_BYTES
        ),
        name="tail",
    )(normed, cot_rows, partials, gram, basis_query, basis_output)


def body(tokens, segments, norm_gain, q_weight, kv_weight, o_weight, basis_query, basis_output):
    groups = lax.axis_size(DP)
    seq_count, length, model_width = tokens.shape
    row_count = seq_count * length
    col_count = q_weight.shape[1]
    heads_dev = col_count // HD
    group_size = QH // KVH
    qwidth = QH * HD
    query_scale = D ** (-0.5)
    output_scale = qwidth ** (-0.5)
    gn_scale = qwidth / (row_count * groups)
    param_count = 2.0 * D * qwidth
    query, tangent, key_states, values, normed, gram, wall = project(
        tokens.reshape(row_count, model_width),
        norm_gain.reshape(1, model_width),
        q_weight,
        basis_query,
        kv_weight,
        basis_output,
        o_weight,
        param_count,
    )
    allowed = allowed_pairs(segments)
    query_wide = query.astype(jnp.float32).reshape(seq_count, length, heads_dev, HD)
    tangent_wide = tangent.astype(jnp.float32).reshape(seq_count, length, heads_dev, HD)
    key_wide = key_states.astype(jnp.float32).reshape(seq_count, length, HD)
    value_wide = values.astype(jnp.float32).reshape(seq_count, length, HD)

    def attend_here(moving):
        return attend(moving, key_wide, value_wide, allowed)

    heads_out, tangent_heads = jax.jvp(attend_here, (query_wide,), (tangent_wide,))
    heads_out = heads_out.reshape(row_count, col_count).astype(jnp.bfloat16)
    tangent_heads = tangent_heads.reshape(row_count, col_count).astype(jnp.bfloat16)
    heads_out = heads_out * jnp.bfloat16(output_scale)
    both_heads = jnp.concatenate([heads_out, tangent_heads], axis=1)
    cot_heads, partials = output_side(both_heads.reshape(8, 2, 32, 2 * col_count), wall)
    cot_heads = cot_heads.astype(jnp.float32)
    _, pullback = jax.vjp(attend_here, query_wide)
    cot_query = pullback(cot_heads.reshape(seq_count, length, heads_dev, HD))[0]
    cot_query = cot_query.reshape(row_count, col_count).astype(jnp.bfloat16)
    clean_query, clean_output, lines = tail(
        normed,
        cot_query.T,
        partials,
        gram,
        basis_query,
        basis_output,
        gn_scale * query_scale,
        param_count,
    )
    beta = lines[8, 0]
    return (
        (clean_query / beta).astype(jnp.bfloat16),
        (clean_output / beta).astype(jnp.bfloat16),
        lines[:9, 0],
    )


def solution(mesh):
    finer = Mesh(
        mesh.devices.reshape(4, 2, 4, 2, 2), ("dp_0", "dp_1", "tensor_0", "tensor_1", "tensor_2")
    )
    placed = (
        P(DP, None, None),
        P(DP, None),
        P(),
        P(DP, TENSOR),
        P(None, DP, None),
        P(TENSOR, DP),
        P(None, DP, TENSOR),
        P(None, TENSOR, DP),
    )
    return jax.shard_map(
        body,
        mesh=finer,
        in_specs=placed,
        out_specs=(P(DP, TENSOR), P(TENSOR, DP), P()),
        check_vma=False,
    )
```

time: 352 us -> 308 us (0.88)
  Pallas kernels: 328 us -> 281 us
  other arithmetic: 4.49 us -> 9.97 us
    pallas_call x4 -> x3, Pallas kernels: 328 us -> 281 us  [the longest x1 113 us: project(): pl.pallas_call(functools.partial(project_kernel, count), out_shape=(shape...]
    convert_element_type x0 -> x2, other arithmetic: none -> 5.49 us  [the longest x1 2.75 us: body(): (clean_output / beta).astype(jnp.bfloat16)]
    unnamed x5 -> x3, local copies, waits for them, and re-layouts: 4.47 us -> 0.74 us
where the time goes in v3:
time: 308 us; the launch traced here: 307 us
  Pallas kernels  281 us (91%)
  other arithmetic  9.97 us (3%)
  local copies, waits for them, and re-layouts  9.08 us (3%)
  matrix products  6.74 us (2%)
    pallas_call x1, Pallas kernels, project(): pl.pallas_call(functools.partial(project_kernel, count), out_shape=(shape...  113 us
    pallas_call x1, Pallas kernels, tail(): pl.pallas_call(functools.partial(tail_kernel, factor, count), out_shape=(...  89.6 us
    pallas_call x1, Pallas kernels, output_side(): pl.pallas_call(output_kernel, out_shape=(shape((8, 2, 32, 256), BF), shap...  78.6 us

profile of v3, /device:TPU:1, one launch (start us, length us, event | category | flops | bytes accessed | tf_op | source)
XLA Modules:
  0.0 307.4 jit_solution(5771277327940362133)
XLA Ops:
  0.7 1.0 compare_and_fusion.1
  1.7 0.3 copy.27
  2.0 0.5 fusion.38
  2.5 112.6 %project.1 = (bf16[512,256]{1,0:T(8,128)(2,1)}, bf16[512,256]{1,0:T(8,128)(2,1)}, bf16[512,128]{1,0:T(8,128)(2,1)}, bf16[512,128]{1,0:T(8,128)(2,1)}, bf16[512,8...) custom-call(bf16[512,8192]{1,0:T(8,128)(2,1)} %bitcast.88, f32[1,8192]{1,0:T(1,128)} %bitcast.96, ...), custom_call_target="tpu_custom_call" | custom-call | tf_op jit(solution)/shard_map/project/pallas_call | solution.py:411
  115.1 0.9 convert.3
  116.0 0.2 multiply_subtract_fusion.2
  116.2 1.2 reshape.179
  117.4 1.2 reshape.181
  118.6 1.1 fusion.47
  119.8 0.3 multiply_subtract_fusion.1
  120.1 0.0 copy-start
  120.1 1.2 fusion.17
  121.3 0.2 fusion.39
  121.6 1.4 fusion.49
  123.0 0.0 copy-done
  123.0 0.8 fusion.3
  123.8 0.2 copy.37
  124.0 0.2 convert_element_type.36
  124.2 0.7 fusion.5
  124.9 0.2 copy.32
  125.1 0.2 mul.415
  125.3 0.8 pad_maximum_fusion.h
  126.1 78.6 %output_side.1 = (bf16[8,2,32,256]{3,2,1,0:T(8,128)(2,1)}, bf16[2,4,2,256,512]{4,3,2,1,0:T(8,128)(2,1)}) custom-call(bf16[8,2,32,512]{3,2,1,0:T(8,128)(2,1)} %pad_maximum_fusion.h, bf16[2,8,256,1024]{3,2,1,0:T(8,128)(2,1)} %get-tuple-element.20.wall), custom_call_target="tpu_custom_call" | custom-call | tf_op jit(solution)/shard_map/output_side/pallas_call | solution.py:606
  204.7 1.0 reshape.175
  205.7 0.1 copy.38
  205.9 0.4 multiply_reduce_fusion
  206.3 2.1 fusion.15
  208.4 0.2 multiply_add_fusion.1
  208.7 0.2 add_convert_fusion
  208.9 0.2 copy.42
  209.1 0.7 copy.61
  209.8 89.6 %tail.1 = (f32[1024,256]{1,0:T(8,128)}, f32[256,1024]{1,0:T(8,128)}, f32[16,128]{1,0:T(8,128)}) custom-call(bf16[512,8192]{1,0:T(8,128)(2,1)} %get-tuple-element.15.normed_hbm, bf16[256,512]{1,0:T(8,128)(2,1)} %bitcast.89, bf16[2,4,2,256,512]{4,3,2,1,0:T(8,128)(2,1)} %get-tuple-element.22.gp, f32[8,128]{1,0:T(8,128)} %get-tuple-element.23.gram, ...), custom_call_target="tpu_custom_call" | custom-call | tf_op jit(solution)/shard_map/tail/pallas_call | solution.py:839
  299.4 1.2 slice.34
  300.6 2.7 divide_convert_fusion.1
  303.4 2.8 divide_convert_fusion
  306.1 1.3 slice_reduce_fusion
  (5 shorter events, 0.1 us)
Async XLA Ops:
  120.1 2.9 copy-start

commit v4 on v3

--- a/solution.py
+++ b/solution.py
@@ -55,7 +55,10 @@
     barrier = pltpu.get_barrier_semaphore()
     for masks in peers:
         pl.semaphore_signal(barrier, inc=1, device_id=peer(here, masks), device_id_type=MESH)
-    pl.semaphore_wait(barrier, len(peers))
+
+
+def greeted(peers):
+    pl.semaphore_wait(pltpu.get_barrier_semaphore(), len(peers))
 
 
 def send(src, dst, send_sem, recv_sem, here, masks):
@@ -88,8 +91,10 @@
 OUT_STAGES = ((YL, Z1, Z3), (YL, Z3, Z1))
 
 
-DP_PEERS = [(x, yh, 0, 0, 0) for x in range(4) for yh in range(2) if x or yh]
-TENSOR_PEERS = [(0, 0, z, yl, c) for z in range(4) for yl in range(2) for c in range(2) if z or yl or c]
+XY_PEERS = [
+    (x, yh, 0, yl, 0) for x in range(4) for yh in range(2) for yl in range(2) if x or yh or yl
+]
+ZC_PEERS = [(0, 0, z, 0, c) for z in range(4) for c in range(2) if z or c]
 
 
 def z_place(mask, kind):
@@ -115,33 +120,59 @@
     return (jnp.cos(angles), jnp.sin(angles))
 
 
-def rotate(vectors, cosine_table, sine_table):
-    half_width = vectors.shape[-1] // 2
-    front_half = vectors[..., :half_width]
-    back_half = vectors[..., half_width:]
-    return jnp.concatenate(
-        [
-            front_half * cosine_table - back_half * sine_table,
-            front_half * sine_table + back_half * cosine_table,
-        ],
-        axis=-1,
+def rotated(vectors, cos_twice, sin_signed):
+    return vectors * cos_twice + pltpu.roll(vectors, HD // 2, 1) * sin_signed
+
+
+def rotated_back(vectors, cos_twice, sin_signed):
+    return vectors * cos_twice - pltpu.roll(vectors, HD // 2, 1) * sin_signed
+
+
+def dot_wide(a, b, a_dim, b_dim):
+    return lax.dot_general(
+        a, b, (((a_dim,), (b_dim,)), ((), ())), precision=PRECISE, preferred_element_type=F32
     )
 
 
-def attend(query, key_states, values, allowed):
-    length = query.shape[1]
-    head_width = query.shape[-1]
-    cosine_table, sine_table = rope_tables(length, head_width)
-    query = rotate(query, cosine_table[:, None, :], sine_table[:, None, :])
-    key_states = rotate(key_states, cosine_table, sine_table)
-    scores = jnp.einsum("slgd,smd->sglm", query, key_states, precision=PRECISE) * head_width ** (
-        -0.5
-    )
-    scores = jnp.where(allowed[:, None, :, :], scores, -1e30)
-    row_max = lax.stop_gradient(jnp.max(scores, axis=-1, keepdims=True))
-    weights = jnp.exp(scores - row_max)
-    probabilities = weights / jnp.sum(weights, axis=-1, keepdims=True)
-    return jnp.einsum("sglm,smd->slgd", probabilities, values, precision=PRECISE)
+def attend_both(q, t, k, v, allowed, cos_twice, sin_signed, h, probs):
+    scale = HD ** (-0.5)
+    for s in range(2):
+        rows = pl.ds(s * 256, 256)
+        keys = rotated(k[rows].astype(F32), cos_twice[...], sin_signed[...])
+        values = v[rows].astype(F32)
+        mask = allowed[s].astype(F32) > 0.5
+        for head in range(2):
+            cols = pl.ds(head * HD, HD)
+            moving = rotated(q[rows, cols].astype(F32), cos_twice[...], sin_signed[...])
+            along = rotated(t[rows, cols].astype(F32), cos_twice[...], sin_signed[...])
+            scores = jnp.where(mask, dot_wide(moving, keys, 1, 1) * scale, -1e30)
+            weights = jnp.exp(scores - jnp.max(scores, axis=1, keepdims=True))
+            p = weights / jnp.sum(weights, axis=1, keepdims=True)
+            probs[2 * s + head] = p
+            slope = jnp.where(mask, dot_wide(along, keys, 1, 1) * scale, 0.0)
+            dp = p * (slope - jnp.sum(p * slope, axis=1, keepdims=True))
+            heads = dot_wide(p, values, 1, 0).astype(BF).astype(F32) * ((QH * HD) ** (-0.5))
+            tangents = dot_wide(dp, values, 1, 0)
+            h[pl.ds(4 * s, 4), :, :, cols] = heads.astype(BF).reshape(4, 2, 32, HD)
+            h[pl.ds(4 * s, 4), :, :, pl.ds(256 + head * HD, HD)] = tangents.astype(BF).reshape(
+                4, 2, 32, HD
+            )
+
+
+def attend_back(cot, k, v, probs, cos_twice, sin_signed, out):
+    scale = HD ** (-0.5)
+    for s in range(2):
+        rows = pl.ds(s * 256, 256)
+        keys = rotated(k[rows].astype(F32), cos_twice[...], sin_signed[...])
+        values = v[rows].astype(F32)
+        for head in range(2):
+            cols = pl.ds(head * HD, HD)
+            given = cot[pl.ds(4 * s, 4), :, :, cols].reshape(256, HD).astype(F32)
+            p = probs[2 * s + head]
+            slope = dot_wide(given, values, 1, 1)
+            ds = p * (slope - jnp.sum(p * slope, axis=1, keepdims=True))
+            moving = rotated_back(dot_wide(ds, keys, 1, 0) * scale, cos_twice[...], sin_signed[...])
+            out[cols, rows] = moving.T.astype(BF)
 
 
 def allowed_pairs(segments):
@@ -181,7 +212,8 @@
         copy = pltpu.make_async_copy(src, w.at[kind, 0], load.at[16 + kind])
         copy.start()
         own_out.append(copy)
-    greet(here, DP_PEERS + TENSOR_PEERS)
+    greet(here, XY_PEERS + ZC_PEERS)
+    greeted(XY_PEERS + ZC_PEERS)
     for copy in for_rows:
         copy.wait()
 
@@ -238,8 +270,8 @@
         copy.start()
         wall_copies.append(copy)
 
-    dp = here[0] * 2 + here[1]
-    tensor = here[2] * 4 + here[3] * 2 + here[4]
+    xy_own = here[0] * 4 + here[1] * 2 + here[3]
+    zc_own = here[2] * 2 + here[4]
 
     def exchange(slots, own, peers, base):
         ref = slots.at[own]
@@ -308,7 +340,7 @@
                 jnp.logical_and(lane == i, row == j), jnp.logical_and(lane == j, row == i)
             )
             tile_sum = tile_sum + jnp.where(hit, value, 0.0)
-        g1[dp] = tile_sum
+        g1[xy_own] = tile_sum
 
     acc[...] = jnp.zeros_like(acc)
     second, third = [], []
@@ -338,7 +370,7 @@
             vq_copy.wait()
             vo_copy.wait()
             gram()
-            over_dp = exchange(g1, dp, DP_PEERS, 73)
+            over_xy = exchange(g1, xy_own, XY_PEERS, 73)
         if k == 8:
             dots(0, 0, 4)
         if k == 9:
@@ -346,13 +378,13 @@
         if k == 10:
             keep_wall(0, 0)
             keep_wall(1, 0)
-            for copy in over_dp:
+            for copy in over_xy:
                 copy.wait_recv()
             total = g1[0]
-            for n in range(1, 8):
+            for n in range(1, 16):
                 total = total + g1[n]
-            g2[tensor] = total
-            over_tensor = exchange(g2, tensor, TENSOR_PEERS, 80)
+            g2[zc_own] = total
+            over_zc = exchange(g2, zc_own, ZC_PEERS, 88)
         if k == 13:
             for n in (0, 2, 4, 6):
                 third[n].wait_recv()
@@ -385,13 +417,13 @@
         for piece in range(4):
             out_copies[2, kind, piece].wait_recv()
         keep_wall(kind, 4)
-    for copy in over_tensor:
+    for copy in over_zc:
         copy.wait_recv()
     total = g2[0]
-    for n in range(1, 16):
+    for n in range(1, 8):
         total = total + g2[n]
     gram_out[...] = total / count
-    for copy in first + second + third + list(out_copies.values()) + over_dp + over_tensor:
+    for copy in first + second + third + list(out_copies.values()) + over_xy + over_zc:
         copy.wait_send()
     for copy in wall_copies:
         copy.wait()
@@ -430,8 +462,8 @@
             pltpu.VMEM((K, 1024, 256), BF),
             pltpu.VMEM((K, 256, 1024), BF),
             pltpu.VMEM((2, 8, 256, 1024), BF),
+            pltpu.VMEM((16, 8, 128), F32),
             pltpu.VMEM((8, 8, 128), F32),
-            pltpu.VMEM((16, 8, 128), F32),
             pltpu.SemaphoreType.DMA((22,)),
             pltpu.SemaphoreType.DMA((95,)),
             pltpu.SemaphoreType.DMA((95,)),
@@ -444,8 +476,8 @@
 
 
 def output_kernel(
-    h, wall, cot, gp_out,
-    w, g, acc, tb, mine, theirs, cs, c1, c2, c3, gp, load, sent, got,
+    q, t, k, v, allowed, cos_twice, sin_signed, wall, cot, gp_out, probs,
+    h, w, g, acc, tb, mine, theirs, cs, c1, c2, c3, gp, load, sent, got,
 ):
     here = position()
     place = here[2] * 2 + here[3]
@@ -454,7 +486,10 @@
         copy = pltpu.make_async_copy(wall.at[kind], w.at[kind], load.at[kind])
         copy.start()
         loads.append(copy)
-    greet(here, [X1, X3, YH, CORE] + [same_core_masks(r) for r in range(1, 8)])
+    peers = [X1, X3, YH, CORE] + [same_core_masks(r) for r in range(1, 8)]
+    greet(here, peers)
+    attend_both(q, t, k, v, allowed, cos_twice, sin_signed, h, probs)
+    greeted(peers)
     copies = []
 
     def start(at, src, dst, masks):
@@ -601,14 +636,19 @@
     gp_copy.wait()
 
 
-def output_side(heads, wall):
+def output_side(query, tangent, key_states, values, allowed, cos_twice, sin_signed, wall):
     shape = jax.ShapeDtypeStruct
     return pl.pallas_call(
         output_kernel,
-        out_shape=(shape((8, 2, 32, 256), BF), shape((2, 4, 2, 256, 512), BF)),
-        in_specs=vmem_specs(1) + any_specs(1),
-        out_specs=tuple(vmem_specs(1) + any_specs(1)),
+        out_shape=(
+            shape((8, 2, 32, 256), BF),
+            shape((2, 4, 2, 256, 512), BF),
+            shape((4, 256, 256), F32),
+        ),
+        in_specs=vmem_specs(7) + any_specs(1),
+        out_specs=tuple(vmem_specs(1) + any_specs(1) + vmem_specs(1)),
         scratch_shapes=[
+            pltpu.VMEM((8, 2, 32, 512), BF),
             pltpu.VMEM((2, 8, 256, 1024), BF),
             pltpu.VMEM((2, 8, 8, 32, 512), BF),
             pltpu.VMEM((512, 1024), F32),
@@ -628,17 +668,17 @@
             collective_id=3, has_side_effects=True, vmem_limit_bytes=VMEM_BYTES
         ),
         name="output_side",
-    )(heads, wall)
+    )(query, tangent, key_states, values, allowed, cos_twice, sin_signed, wall)
 
 
 def tail_kernel(
-    factor, count, normed_hbm, cot, gp, gram, vec_q, vec_o, clean_q, clean_o, coeffs,
-    normed, part, r1, r2, r3, own, z1, z2, y1, vq, vo, gq, go, facc,
+    factor, count, normed_hbm, cot_heads, k, v, probs, cos_twice, sin_signed, gp, gram, vec_q, vec_o,
+    next_q, next_o, coeffs, cot, normed, part, r1, r2, r3, own, z1, z2, y1, vq, vo, gq, go, facc,
     s1, s2, u1, u2, load, sent, got,
 ):
     here = position()
-    dp = here[0] * 2 + here[1]
-    tensor = here[2] * 4 + here[3] * 2 + here[4]
+    xy_own = here[0] * 4 + here[1] * 2 + here[3]
+    zc_own = here[2] * 2 + here[4]
     loads = []
 
     def fetch(src, dst):
@@ -648,7 +688,8 @@
 
     fetch(gp, own)
     fetch(normed_hbm, normed)
-    greet(here, DP_PEERS + TENSOR_PEERS)
+    greet(here, XY_PEERS + ZC_PEERS)
+    greeted(XY_PEERS + ZC_PEERS)
     copies = []
 
     def keep(copy):
@@ -672,6 +713,8 @@
     def out_low(j):
         kind, rows = j % 2, rows_at(j)
         z_high[j].wait_recv()
+        if j + 4 < 8:
+            out_high(j + 4)
         own[kind, pl.ds(0, 2), :, rows] = (
             own[kind, pl.ds(0, 2), :, rows].astype(F32) + z1[kind, :, :, rows].astype(F32)
         ).astype(BF)
@@ -729,8 +772,9 @@
         one[c] = start(0, c, part.at[c, pl.ds(4, 4)], r1.at[c])
 
     loads[0].wait()
-    for j in range(8):
+    for j in range(4):
         out_high(j)
+    attend_back(cot_heads, k, v, probs, cos_twice, sin_signed, cot)
     loads[1].wait()
     fetch(vec_q, vq)
     fetch(vec_o, vo)
@@ -738,12 +782,12 @@
     product(1, 1, 1)
     product(0, 0, 1)
     product(0, 1, 1)
-    for c in (0, 2, 4, 6):
-        q_one(c)
+    q_one(0)
+    q_one(2)
     product(1, 0, 0)
     product(1, 1, 0)
-    for c in (1, 3, 5, 7):
-        q_one(c)
+    q_one(1)
+    q_one(3)
     product(0, 0, 0)
     product(0, 1, 0)
     facc[...] = jnp.zeros_like(facc)
@@ -755,6 +799,8 @@
 
     def q_two(c):
         one[c].wait_recv()
+        if c + 4 < 8:
+            q_one(c + 4)
         added(c, 4, r1)
         two[c] = start(1, c, part.at[c, pl.ds(2, 2)], r2.at[c])
 
@@ -769,8 +815,8 @@
         gq[pl.ds(c * 128, 128), :] = total.T
         against(gq, vq, c * 128, 8, 0, 2)
 
-    lagged = ((q_two, 0), (out_low, 0), (q_three, 1), (out_y, 1), (q_end, 2), (out_end, 2))
-    for n in range(8 + 2):
+    lagged = ((q_two, 0), (q_three, 2), (out_low, 1), (out_y, 3), (q_end, 4), (out_end, 5))
+    for n in range(8 + 5):
         if n == 2:
             loads[2].wait()
             loads[3].wait()
@@ -785,22 +831,22 @@
             for n, masks in enumerate(peers)
         ]
 
-    def sum_over(over_dp, over_tensor, base):
-        for copy in exchange(over_dp, dp, DP_PEERS, base):
+    def sum_over(over_xy, over_zc, base):
+        for copy in exchange(over_xy, xy_own, XY_PEERS, base):
             copy.wait_recv()
-        total = over_dp[0]
+        total = over_xy[0]
+        for n in range(1, 16):
+            total = total + over_xy[n]
+        over_zc[zc_own] = total
+        for copy in exchange(over_zc, zc_own, ZC_PEERS, base + 15):
+            copy.wait_recv()
+        total = over_zc[0]
         for n in range(1, 8):
-            total = total + over_dp[n]
-        over_tensor[tensor] = total
-        for copy in exchange(over_tensor, tensor, TENSOR_PEERS, base + 7):
-            copy.wait_recv()
-        total = over_tensor[0]
-        for n in range(1, 16):
-            total = total + over_tensor[n]
+            total = total + over_zc[n]
         return total
 
     for j in range(K):
-        s1[dp, pl.ds(j, 1)] = jnp.sum(facc[j], axis=0, keepdims=True)
+        s1[xy_own, pl.ds(j, 1)] = jnp.sum(facc[j], axis=0, keepdims=True)
     first = jnp.sum(sum_over(s1, s2, 48), axis=1, keepdims=True) / count
     second = first
     for i in range(K):
@@ -823,25 +869,32 @@
 
         return lax.fori_loop(0, row_tiles, step, state)
 
-    state = cleaned(gq, vq, clean_q, 64, 2, jnp.zeros((8, 128), F32))
-    u1[dp] = cleaned(go, vo, clean_o, 16, 8, state)
+    state = cleaned(gq, vq, gq, 64, 2, jnp.zeros((8, 128), F32))
+    u1[xy_own] = cleaned(go, vo, go, 16, 8, state)
     squares = sum_over(u1, u2, 70)
     squares = jnp.sum(jnp.sum(squares, axis=1, keepdims=True), axis=0, keepdims=True) / count
     beta = jnp.sqrt(squares + BETA_EPS)
+    scale = 1.0 / beta
+    next_q[...] = (gq[...] * scale).astype(BF)
+    next_o[...] = (go[...] * scale).astype(BF)
     coeffs[pl.ds(0, 8)] = jnp.broadcast_to(both, (8, 128))
     coeffs[pl.ds(8, 8)] = jnp.broadcast_to(beta, (8, 128))
     for copy in copies:
         copy.wait_send()
 
 
-def tail(normed, cot_rows, partials, gram, basis_query, basis_output, factor, count):
+def tail(
+    normed, cot_heads, key_states, values, probs, cos_twice, sin_signed,
+    partials, gram, basis_query, basis_output, factor, count,
+):
     shape = jax.ShapeDtypeStruct
     return pl.pallas_call(
         functools.partial(tail_kernel, factor, count),
-        out_shape=(shape((1024, 256), F32), shape((256, 1024), F32), shape((16, 128), F32)),
-        in_specs=any_specs(1) + vmem_specs(1) + any_specs(1) + vmem_specs(1) + any_specs(2),
+        out_shape=(shape((1024, 256), BF), shape((256, 1024), BF), shape((16, 128), F32)),
+        in_specs=any_specs(1) + vmem_specs(6) + any_specs(1) + vmem_specs(1) + any_specs(2),
         out_specs=tuple(vmem_specs(3)),
         scratch_shapes=[
+            pltpu.VMEM((256, 512), BF),
             pltpu.VMEM((512, D), BF),
             pltpu.VMEM((8, 8, 256, 128), BF),
             pltpu.VMEM((8, 4, 256, 128), BF),
@@ -856,10 +909,10 @@
             pltpu.VMEM((1024, 256), F32),
             pltpu.VMEM((256, 1024), F32),
             pltpu.VMEM((K, 8, 128), F32),
+            pltpu.VMEM((16, 8, 128), F32),
             pltpu.VMEM((8, 8, 128), F32),
             pltpu.VMEM((16, 8, 128), F32),
             pltpu.VMEM((8, 8, 128), F32),
-            pltpu.VMEM((16, 8, 128), F32),
             pltpu.SemaphoreType.DMA((4,)),
             pltpu.SemaphoreType.DMA((92,)),
             pltpu.SemaphoreType.DMA((92,)),
@@ -868,19 +921,18 @@
             collective_id=1, has_side_effects=True, vmem_limit_bytes=VMEM_BYTES
         ),
         name="tail",
-    )(normed, cot_rows, partials, gram, basis_query, basis_output)
+    )(
+        normed, cot_heads, key_states, values, probs, cos_twice, sin_signed,
+        partials, gram, basis_query, basis_output,
+    )
 
 
 def body(tokens, segments, norm_gain, q_weight, kv_weight, o_weight, basis_query, basis_output):
     groups = lax.axis_size(DP)
     seq_count, length, model_width = tokens.shape
     row_count = seq_count * length
-    col_count = q_weight.shape[1]
-    heads_dev = col_count // HD
-    group_size = QH // KVH
     qwidth = QH * HD
     query_scale = D ** (-0.5)
-    output_scale = qwidth ** (-0.5)
     gn_scale = qwidth / (row_count * groups)
     param_count = 2.0 * D * qwidth
     query, tangent, key_states, values, normed, gram, wall = project(
@@ -893,28 +945,21 @@
         o_weight,
         param_count,
     )
-    allowed = allowed_pairs(segments)
-    query_wide = query.astype(jnp.float32).reshape(seq_count, length, heads_dev, HD)
-    tangent_wide = tangent.astype(jnp.float32).reshape(seq_count, length, heads_dev, HD)
-    key_wide = key_states.astype(jnp.float32).reshape(seq_count, length, HD)
-    value_wide = values.astype(jnp.float32).reshape(seq_count, length, HD)
-
-    def attend_here(moving):
-        return attend(moving, key_wide, value_wide, allowed)
-
-    heads_out, tangent_heads = jax.jvp(attend_here, (query_wide,), (tangent_wide,))
-    heads_out = heads_out.reshape(row_count, col_count).astype(jnp.bfloat16)
-    tangent_heads = tangent_heads.reshape(row_count, col_count).astype(jnp.bfloat16)
-    heads_out = heads_out * jnp.bfloat16(output_scale)
-    both_heads = jnp.concatenate([heads_out, tangent_heads], axis=1)
-    cot_heads, partials = output_side(both_heads.reshape(8, 2, 32, 2 * col_count), wall)
-    cot_heads = cot_heads.astype(jnp.float32)
-    _, pullback = jax.vjp(attend_here, query_wide)
-    cot_query = pullback(cot_heads.reshape(seq_count, length, heads_dev, HD))[0]
-    cot_query = cot_query.reshape(row_count, col_count).astype(jnp.bfloat16)
-    clean_query, clean_output, lines = tail(
+    allowed = allowed_pairs(segments).astype(jnp.bfloat16)
+    cosine, sine = rope_tables(length, HD)
+    cos_twice = jnp.concatenate([cosine, cosine], axis=1)
+    sin_signed = jnp.concatenate([-sine, sine], axis=1)
+    cot_heads, partials, probs = output_side(
+        query, tangent, key_states, values, allowed, cos_twice, sin_signed, wall
+    )
+    next_query, next_output, lines = tail(
         normed,
-        cot_query.T,
+        cot_heads,
+        key_states,
+        values,
+        probs,
+        cos_twice,
+        sin_signed,
         partials,
         gram,
         basis_query,
@@ -922,12 +967,7 @@
         gn_scale * query_scale,
         param_count,
     )
-    beta = lines[8, 0]
-    return (
-        (clean_query / beta).astype(jnp.bfloat16),
-        (clean_output / beta).astype(jnp.bfloat16),
-        lines[:9, 0],
-    )
+    return (next_query, next_output, lines[:9, 0])
 
 
 def solution(mesh):

time: 308 us -> 281 us (0.912)
  Pallas kernels: 281 us -> 272 us
  other arithmetic: 9.97 us -> 3.01 us
  matrix products: 6.74 us -> 0 us
  local copies, waits for them, and re-layouts: 9.08 us -> 5.06 us
    pallas_call x1, Pallas kernels: 89.6 us -> 76.6 us  [tail(): pl.pallas_call(functools.partial(tail_kernel, factor, count), out_shape=(...]
    dot_general x6 -> x0, matrix products: 6.74 us -> none  [the longest x3 4.77 us: attend(): jnp.einsum('slgd,smd->sglm', query, key_states, precision=PRECISE)]
    pallas_call x1, Pallas kernels: 78.6 us -> 83.5 us  [output_side(): pl.pallas_call(output_kernel, out_shape=(shape((8, 2, 32, 256), BF), shap...]
    convert_element_type x3 -> x1, other arithmetic: 5.7 us -> 1.61 us  [body(): allowed = allowed_pairs(segments).astype(jnp.bfloat16)]
    reshape x4 -> x0, local copies, waits for them, and re-layouts: 3.57 us -> none  [the longest x1 1.21 us: body(): query.astype(jnp.float32).reshape(seq_count, length, heads_dev, HD)]
where the time goes in v4:
time: 281 us
  Pallas kernels  272 us (97%)
  local copies, waits for them, and re-layouts  5.06 us (2%)
  other arithmetic  3.01 us (1%)
    pallas_call x1, Pallas kernels, project(): pl.pallas_call(functools.partial(project_kernel, count), out_shape=(shape...  112 us
    pallas_call x1, Pallas kernels, output_side(): pl.pallas_call(output_kernel, out_shape=(shape((8, 2, 32, 256), BF), shap...  83.5 us
    pallas_call x1, Pallas kernels, tail(): pl.pallas_call(functools.partial(tail_kernel, factor, count), out_shape=(...  76.6 us

profile of v4, /device:TPU:1, one launch (start us, length us, event | category | flops | bytes accessed | tf_op | source)
XLA Modules:
  0.0 280.8 jit_solution(11597363560913262698)
XLA Ops:
  0.7 1.6 and_convert_fusion.allowed
  2.3 0.5 fusion.2
  2.8 0.8 pad_maximum_fusion
  3.6 112.0 %project.1 = (bf16[512,256]{1,0:T(8,128)(2,1)}, bf16[512,256]{1,0:T(8,128)(2,1)}, bf16[512,128]{1,0:T(8,128)(2,1)}, bf16[512,128]{1,0:T(8,128)(2,1)}, bf16[512,8...) custom-call(bf16[512,8192]{1,0:T(8,128)(2,1)} %bitcast.2, f32[1,8192]{1,0:T(1,128)} %bitcast.3, ...), custom_call_target="tpu_custom_call" | custom-call | tf_op jit(solution)/shard_map/project/pallas_call | solution.py:443
  115.6 83.5 %output_side.1 = (bf16[8,2,32,256]{3,2,1,0:T(8,128)(2,1)}, bf16[2,4,2,256,512]{4,3,2,1,0:T(8,128)(2,1)}, f32[4,256,256]{2,1,0:T(8,128)}) custom-call(bf16[512,256]{1,0:T(8,128)(2,1)} %get-tuple-element.17.q, bf16[512,256]{1,0:T(8,128)(2,1)} %get-tuple-element.18.t, bf16[512,128]{1,0:T(8,128)(2,1)} %get-tuple-element.19.k, ...), custom_call_target="tpu_custom_call" | custom-call | tf_op jit(solution)/shard_map/output_side/pallas_call | solution.py:641
  199.1 76.6 %tail.1 = (bf16[1024,256]{1,0:T(8,128)(2,1)}, bf16[256,1024]{1,0:T(8,128)(2,1)}, f32[16,128]{1,0:T(8,128)}) custom-call(bf16[512,8192]{1,0:T(8,128)(2,1)} %get-tuple-element.16.normed_hbm, bf16[8,2,32,256]{3,2,1,0:T(8,128)(2,1)} %get-tuple-element.22.cot_heads, bf16[512,128]{1,0:T(8,128)(2,1)} %get-tuple-element.19.k, bf16[512,128]{1,0:T(8,128)(2,1)} %get-tuple-element.20.v, ...), custom_call_target="tpu_custom_call" | custom-call | tf_op jit(solution)/shard_map/tail/pallas_call | solution.py:891
  275.7 1.3 slice_reduce_fusion
  277.1 1.9 copy.13
  278.9 1.9 copy.14
  (2 shorter events, 0.0 us)

commit v5 on v4

--- a/solution.py
+++ b/solution.py
@@ -3,6 +3,7 @@
 
 import jax
 import jax.numpy as jnp
+import numpy as np
 from jax import lax
 from jax.experimental import pallas as pl
 from jax.experimental.pallas import tpu as pltpu
@@ -113,11 +114,12 @@
 
 def rope_tables(length, head_width):
     half_width = head_width // 2
-    frequency = jnp.exp(
-        jnp.arange(half_width, dtype=jnp.float32) * (-2.0 * math.log(ROPE_BASE) / head_width)
-    )
-    angles = jnp.arange(length, dtype=jnp.float32)[:, None] * frequency[None, :]
-    return (jnp.cos(angles), jnp.sin(angles))
+    frequency = np.exp(
+        np.arange(half_width, dtype=np.float32) * np.float32(-2.0 * math.log(ROPE_BASE) / head_width)
+    ).astype(np.float32)
+    angles = np.arange(length, dtype=np.float32)[:, None] * frequency[None, :]
+    cosine, sine = np.cos(angles), np.sin(angles)
+    return (np.concatenate([cosine, cosine], axis=1), np.concatenate([-sine, sine], axis=1))
 
 
 def rotated(vectors, cos_twice, sin_signed):
@@ -134,29 +136,29 @@
     )
 
 
-def attend_both(q, t, k, v, allowed, cos_twice, sin_signed, h, probs):
+def attend_both(s, q, t, k, v, segments, cos_twice, sin_signed, h, probs):
     scale = HD ** (-0.5)
-    for s in range(2):
-        rows = pl.ds(s * 256, 256)
-        keys = rotated(k[rows].astype(F32), cos_twice[...], sin_signed[...])
-        values = v[rows].astype(F32)
-        mask = allowed[s].astype(F32) > 0.5
-        for head in range(2):
-            cols = pl.ds(head * HD, HD)
-            moving = rotated(q[rows, cols].astype(F32), cos_twice[...], sin_signed[...])
-            along = rotated(t[rows, cols].astype(F32), cos_twice[...], sin_signed[...])
-            scores = jnp.where(mask, dot_wide(moving, keys, 1, 1) * scale, -1e30)
-            weights = jnp.exp(scores - jnp.max(scores, axis=1, keepdims=True))
-            p = weights / jnp.sum(weights, axis=1, keepdims=True)
-            probs[2 * s + head] = p
-            slope = jnp.where(mask, dot_wide(along, keys, 1, 1) * scale, 0.0)
-            dp = p * (slope - jnp.sum(p * slope, axis=1, keepdims=True))
-            heads = dot_wide(p, values, 1, 0).astype(BF).astype(F32) * ((QH * HD) ** (-0.5))
-            tangents = dot_wide(dp, values, 1, 0)
-            h[pl.ds(4 * s, 4), :, :, cols] = heads.astype(BF).reshape(4, 2, 32, HD)
-            h[pl.ds(4 * s, 4), :, :, pl.ds(256 + head * HD, HD)] = tangents.astype(BF).reshape(
-                4, 2, 32, HD
-            )
+    rows = pl.ds(s * 256, 256)
+    keys = rotated(k[rows].astype(F32), cos_twice[...], sin_signed[...])
+    values = v[rows].astype(F32)
+    across = jnp.broadcast_to(segments[pl.ds(s, 1)].astype(F32), (256, 256))
+    row = lax.broadcasted_iota(jnp.int32, (256, 256), 0)
+    column = lax.broadcasted_iota(jnp.int32, (256, 256), 1)
+    mask = jnp.logical_and(across == across.T, row >= column)
+    for head in range(2):
+        cols = pl.ds(head * HD, HD)
+        moving = rotated(q[rows, cols].astype(F32), cos_twice[...], sin_signed[...])
+        along = rotated(t[rows, cols].astype(F32), cos_twice[...], sin_signed[...])
+        scores = jnp.where(mask, dot_wide(moving, keys, 1, 1) * scale, -1e30)
+        weights = jnp.exp(scores - jnp.max(scores, axis=1, keepdims=True))
+        p = weights / jnp.sum(weights, axis=1, keepdims=True)
+        probs[2 * s + head] = p
+        slope = jnp.where(mask, dot_wide(along, keys, 1, 1) * scale, 0.0)
+        dp = p * (slope - jnp.sum(p * slope, axis=1, keepdims=True))
+        heads = dot_wide(p, values, 1, 0).astype(BF).astype(F32) * ((QH * HD) ** (-0.5))
+        tangents = dot_wide(dp, values, 1, 0)
+        h[s, :, :, cols] = heads.astype(BF).reshape(8, 32, HD)
+        h[s, :, :, pl.ds(256 + head * HD, HD)] = tangents.astype(BF).reshape(8, 32, HD)
 
 
 def attend_back(cot, k, v, probs, cos_twice, sin_signed, out):
@@ -167,19 +169,12 @@
         values = v[rows].astype(F32)
         for head in range(2):
             cols = pl.ds(head * HD, HD)
-            given = cot[pl.ds(4 * s, 4), :, :, cols].reshape(256, HD).astype(F32)
+            given = cot[s, :, :, cols].reshape(256, HD).astype(F32)
             p = probs[2 * s + head]
             slope = dot_wide(given, values, 1, 1)
             ds = p * (slope - jnp.sum(p * slope, axis=1, keepdims=True))
             moving = rotated_back(dot_wide(ds, keys, 1, 0) * scale, cos_twice[...], sin_signed[...])
             out[cols, rows] = moving.T.astype(BF)
-
-
-def allowed_pairs(segments):
-    length = segments.shape[1]
-    position = jnp.arange(length, dtype=jnp.int32)
-    causal = position[:, None] >= position[None, :]
-    return jnp.logical_and(segments[:, :, None] == segments[:, None, :], causal[None])
 
 
 SUPER = (0, 1) * 4 + (2, 3) * 4
@@ -476,7 +471,7 @@
 
 
 def output_kernel(
-    q, t, k, v, allowed, cos_twice, sin_signed, wall, cot, gp_out, probs,
+    q, t, k, v, segments, cos_twice, sin_signed, wall, cot, gp_out, probs,
     h, w, g, acc, tb, mine, theirs, cs, c1, c2, c3, gp, load, sent, got,
 ):
     here = position()
@@ -488,8 +483,6 @@
         loads.append(copy)
     peers = [X1, X3, YH, CORE] + [same_core_masks(r) for r in range(1, 8)]
     greet(here, peers)
-    attend_both(q, t, k, v, allowed, cos_twice, sin_signed, h, probs)
-    greeted(peers)
     copies = []
 
     def start(at, src, dst, masks):
@@ -501,11 +494,16 @@
         z, yl = peer(here[2:4], same_core_masks(r)[2:4])
         return z * 2 + yl
 
-    spread = {
-        r: start(r, h.at[index_of(r)], g.at[:, r, 0], same_core_masks(r)) for r in range(1, 8)
-    }
-    g[:, 0, 0] = h[place]
-
+    spread = {}
+    for kind in range(2):
+        attend_both(kind, q, t, k, v, segments, cos_twice, sin_signed, h, probs)
+        if kind == 0:
+            greeted(peers)
+        for r in range(1, 8):
+            spread[r, kind] = start(
+                (0, 66)[kind] + r, h.at[kind, index_of(r)], g.at[kind, r, 0], same_core_masks(r)
+            )
+        g[kind, 0, 0] = h[kind, place]
     def gather(stage, rg, kind):
         n = 1 << stage
         group = pl.ds(rg * 2, 2)
@@ -517,11 +515,11 @@
         )
 
     one, two, three = {}, {}, {}
-    for rg in range(4):
-        for r in (rg * 2, rg * 2 + 1):
-            if r:
-                spread[r].wait_recv()
-        for kind in range(2):
+    for kind in range(2):
+        for rg in range(4):
+            for r in (rg * 2, rg * 2 + 1):
+                if r:
+                    spread[r, kind].wait_recv()
             one[rg, kind] = gather(0, rg, kind)
     order = [(rg, kind) for rg in range(4) for kind in range(2)]
     for n, key in enumerate(order):
@@ -625,8 +623,8 @@
             added((rg, kind), 1, c3)
         for r in (rg * 2, rg * 2 + 1):
             if r:
-                back[r] = start(r + 58, cs.at[:, r, 0], cot.at[place], same_core_masks(r))
-    cot[place] = cs[:, 0, 0]
+                back[r] = start(r + 58, cs.at[:, r, 0], cot.at[:, place], same_core_masks(r))
+    cot[:, place] = cs[:, 0, 0]
     gp_copy = pltpu.make_async_copy(gp, gp_out, load.at[2])
     gp_copy.start()
     for r in range(1, 8):
@@ -636,19 +634,19 @@
     gp_copy.wait()
 
 
-def output_side(query, tangent, key_states, values, allowed, cos_twice, sin_signed, wall):
+def output_side(query, tangent, key_states, values, segments, cos_twice, sin_signed, wall):
     shape = jax.ShapeDtypeStruct
     return pl.pallas_call(
         output_kernel,
         out_shape=(
-            shape((8, 2, 32, 256), BF),
+            shape((2, 8, 32, 256), BF),
             shape((2, 4, 2, 256, 512), BF),
             shape((4, 256, 256), F32),
         ),
         in_specs=vmem_specs(7) + any_specs(1),
         out_specs=tuple(vmem_specs(1) + any_specs(1) + vmem_specs(1)),
         scratch_shapes=[
-            pltpu.VMEM((8, 2, 32, 512), BF),
+            pltpu.VMEM((2, 8, 32, 512), BF),
             pltpu.VMEM((2, 8, 256, 1024), BF),
             pltpu.VMEM((2, 8, 8, 32, 512), BF),
             pltpu.VMEM((512, 1024), F32),
@@ -661,14 +659,14 @@
             pltpu.VMEM((2, 8, 1, 32, 256), BF),
             pltpu.VMEM((2, 4, 2, 256, 512), BF),
             pltpu.SemaphoreType.DMA((3,)),
-            pltpu.SemaphoreType.DMA((66,)),
-            pltpu.SemaphoreType.DMA((66,)),
+            pltpu.SemaphoreType.DMA((74,)),
+            pltpu.SemaphoreType.DMA((74,)),
         ],
         compiler_params=pltpu.CompilerParams(
             collective_id=3, has_side_effects=True, vmem_limit_bytes=VMEM_BYTES
         ),
         name="output_side",
-    )(query, tangent, key_states, values, allowed, cos_twice, sin_signed, wall)
+    )(query, tangent, key_states, values, segments, cos_twice, sin_signed, wall)
 
 
 def tail_kernel(
@@ -927,6 +925,24 @@
     )
 
 
+def finish_kernel(q, o, lines, q_out, o_out, coeffs):
+    q_out[...] = q[...]
+    o_out[...] = o[...]
+    for n in range(K + 1):
+        coeffs[n] = lines[n, 0]
+
+
+def finish(next_query, next_output, lines):
+    shape = jax.ShapeDtypeStruct
+    return pl.pallas_call(
+        finish_kernel,
+        out_shape=(shape((1024, 256), BF), shape((256, 1024), BF), shape((K + 1,), F32)),
+        in_specs=vmem_specs(2) + [pl.BlockSpec(memory_space=pltpu.SMEM)],
+        out_specs=tuple(vmem_specs(2) + [pl.BlockSpec(memory_space=pltpu.SMEM)]),
+        name="finish",
+    )(next_query, next_output, lines)
+
+
 def body(tokens, segments, norm_gain, q_weight, kv_weight, o_weight, basis_query, basis_output):
     groups = lax.axis_size(DP)
     seq_count, length, model_width = tokens.shape
@@ -945,12 +961,9 @@
         o_weight,
         param_count,
     )
-    allowed = allowed_pairs(segments).astype(jnp.bfloat16)
-    cosine, sine = rope_tables(length, HD)
-    cos_twice = jnp.concatenate([cosine, cosine], axis=1)
-    sin_signed = jnp.concatenate([-sine, sine], axis=1)
+    cos_twice, sin_signed = (jnp.asarray(table) for table in rope_tables(length, HD))
     cot_heads, partials, probs = output_side(
-        query, tangent, key_states, values, allowed, cos_twice, sin_signed, wall
+        query, tangent, key_states, values, segments, cos_twice, sin_signed, wall
     )
     next_query, next_output, lines = tail(
         normed,
@@ -967,7 +980,7 @@
         gn_scale * query_scale,
         param_count,
     )
-    return (next_query, next_output, lines[:9, 0])
+    return finish(next_query, next_output, lines)
 
 
 def solution(mesh):

time: 281 us -> 273 us (0.972)
  local copies, waits for them, and re-layouts: 5.06 us -> 0 us
  other arithmetic: 3.01 us -> 0 us
    unnamed x2 -> x0, local copies, waits for them, and re-layouts: 3.73 us -> none
    pallas_call x1 -> x2, Pallas kernels: 83.5 us -> 82.1 us  [the longest x1 79.9 us: output_side(): pl.pallas_call(output_kernel, out_shape=(shape((2, 8, 32, 256), BF), shap...]
where the time goes in v5:
time: 273 us; the launch traced here: 272 us
  Pallas kernels  272 us (100%)
    pallas_call x1, Pallas kernels, project(): pl.pallas_call(functools.partial(project_kernel, count), out_shape=(shape...  112 us
    pallas_call x1, Pallas kernels, output_side(): pl.pallas_call(output_kernel, out_shape=(shape((2, 8, 32, 256), BF), shap...  79.9 us
    pallas_call x1, Pallas kernels, tail(): pl.pallas_call(functools.partial(tail_kernel, factor, count), out_shape=(...  77.4 us

profile of v5, /device:TPU:1, one launch (start us, length us, event | category | flops | bytes accessed | tf_op | source)
XLA Modules:
  0.0 272.4 jit_solution(12109380411936566765)
XLA Ops:
  0.6 112.0 %project.1 = (bf16[512,256]{1,0:T(8,128)(2,1)}, bf16[512,256]{1,0:T(8,128)(2,1)}, bf16[512,128]{1,0:T(8,128)(2,1)}, bf16[512,128]{1,0:T(8,128)(2,1)}, bf16[512,8...) custom-call(bf16[512,8192]{1,0:T(8,128)(2,1)} %bitcast.2, f32[1,8192]{1,0:T(1,128)} %bitcast.3, ...), custom_call_target="tpu_custom_call" | custom-call | tf_op jit(solution)/shard_map/project/pallas_call | solution.py:438
  112.6 79.9 %output_side.1 = (bf16[2,8,32,256]{3,2,1,0:T(8,128)(2,1)}, bf16[2,4,2,256,512]{4,3,2,1,0:T(8,128)(2,1)}, f32[4,256,256]{2,1,0:T(8,128)}) custom-call(bf16[512,256]{1,0:T(8,128)(2,1)} %get-tuple-element.17.q, bf16[512,256]{1,0:T(8,128)(2,1)} %get-tuple-element.18.t, bf16[512,128]{1,0:T(8,128)(2,1)} %get-tuple-element.19.k, ...), custom_call_target="tpu_custom_call" | custom-call | tf_op jit(solution)/shard_map/output_side/pallas_call | solution.py:639
  192.6 77.4 %tail.1 = (bf16[1024,256]{1,0:T(8,128)(2,1)}, bf16[256,1024]{1,0:T(8,128)(2,1)}, f32[16,128]{1,0:T(8,128)}) custom-call(bf16[512,8192]{1,0:T(8,128)(2,1)} %get-tuple-element.16.normed_hbm, bf16[2,8,32,256]{3,2,1,0:T(8,128)(2,1)} %get-tuple-element.22.cot_heads, bf16[512,128]{1,0:T(8,128)(2,1)} %get-tuple-element.19.k, bf16[512,128]{1,0:T(8,128)(2,1)} %get-tuple-element.20.v, ...), custom_call_target="tpu_custom_call" | custom-call | tf_op jit(solution)/shard_map/tail/pallas_call | solution.py:889
  270.0 2.2 finish.1

commit v6 on v5

--- a/solution.py
+++ b/solution.py
@@ -184,7 +184,7 @@
 def project_kernel(
     count, tok, gain, q_w, vec_q, kv_w, vec_o, o_w,
     q_out, t_out, k_out, v_out, normed_out, gram_out, wall,
-    x, buf, acc, mine, theirs, vq, vo, w, g1, g2, load, sent, got,
+    x, buf, acc, mine, theirs, vq, vo, w, g1, g2, pairs_acc, load, sent, got,
 ):
     here = position()
     core = here[4]
@@ -247,9 +247,10 @@
 
     for copy in own_out:
         copy.wait()
-    for kind in range(2):
-        start_out(0, kind, 0)
-    first = [start_stage(0, k) for k in range(16)]
+    for piece in range(2):
+        for kind in range(2):
+            start_out(0, kind, piece)
+    first = [start_stage(0, k) for k in range(6)]
     tok_copy = pltpu.make_async_copy(tok, x, load.at[12])
     tok_copy.start()
     vq_copy = pltpu.make_async_copy(vec_q, vq, load.at[13])
@@ -300,9 +301,9 @@
 
         lax.fori_loop(lo, hi, step, 0)
 
-    def gram():
-        pairs = [(i, j) for i in range(K) for j in range(i, K)]
-
+    pairs = [(i, j) for i in range(K) for j in range(i, K)]
+
+    def gram(part):
         def tile(ref, rows, cols, carry):
             b = [ref[j, rows, cols].astype(F32) for j in range(K)]
             out = []
@@ -323,14 +324,20 @@
                 carry = tile(vo, rows, pl.ds(h * 128, 128), carry)
             return carry
 
-        carry = tuple(jnp.zeros((8, 128), F32) for _ in pairs)
-        carry = lax.fori_loop(0, 64, step_q, carry)
-        carry = lax.fori_loop(0, 16, step_o, carry)
+        carry = tuple(pairs_acc[n] for n in range(len(pairs)))
+        carry = lax.fori_loop(part * 8, part * 8 + 8, step_q, carry)
+        carry = lax.fori_loop(part * 2, part * 2 + 2, step_o, carry)
+        for n, a in enumerate(carry):
+            pairs_acc[n] = a
+
+    def gram_end():
         lane = lax.broadcasted_iota(jnp.int32, (8, 128), 1)
         row = lax.broadcasted_iota(jnp.int32, (8, 128), 0)
         tile_sum = jnp.zeros((8, 128), F32)
-        for (i, j), a in zip(pairs, carry):
-            value = jnp.sum(jnp.sum(a, axis=0, keepdims=True), axis=1, keepdims=True)
+        for n, (i, j) in enumerate(pairs):
+            value = jnp.sum(
+                jnp.sum(pairs_acc[n], axis=0, keepdims=True), axis=1, keepdims=True
+            )
             hit = jnp.logical_or(
                 jnp.logical_and(lane == i, row == j), jnp.logical_and(lane == j, row == i)
             )
@@ -338,6 +345,7 @@
         g1[xy_own] = tile_sum
 
     acc[...] = jnp.zeros_like(acc)
+    pairs_acc[...] = jnp.zeros_like(pairs_acc)
     second, third = [], []
     out_steps = {
         1: (0, 0), 2: (0, 1), 4: (0, 2), 6: (0, 3), 3: (1, 0), 5: (1, 1), 7: (1, 2), 9: (1, 3)
@@ -345,32 +353,37 @@
     for k in range(16):
         first[k].wait_recv()
         second.append(start_stage(1, k))
-        if k >= 1:
-            second[k - 1].wait_recv()
-            third.append(start_stage(2, k - 1))
+        if k + 6 < 16:
+            first.append(start_stage(0, k + 6))
+        if k >= 3:
+            second[k - 3].wait_recv()
+            third.append(start_stage(2, k - 3))
         if k in out_steps:
             stage, piece = out_steps[k]
             next_out(stage, piece)
-        if k in (0, 2, 4):
-            start_out(0, 0, k // 2 + 1)
-            start_out(0, 1, k // 2 + 1)
+        if k in (1, 3):
+            start_out(0, 0, k // 2 + 2)
+            start_out(0, 1, k // 2 + 2)
         if k == 0:
             tok_copy.wait()
-            norm_rows(0, 256)
-        if k == 1:
-            norm_rows(256, 512)
+        if k < 8:
+            norm_rows(k * 64, k * 64 + 64)
+        if k == 7:
             out_copy = pltpu.make_async_copy(x, normed_out, load.at[15])
             out_copy.start()
         if k == 2:
             vq_copy.wait()
             vo_copy.wait()
-            gram()
+        if 2 <= k < 10:
+            gram(k - 2)
+        if k == 10:
+            gram_end()
             over_xy = exchange(g1, xy_own, XY_PEERS, 73)
-        if k == 8:
+        if k == 11:
             dots(0, 0, 4)
-        if k == 9:
+        if k == 12:
             dots(1, 0, 4)
-        if k == 10:
+        if k == 13:
             keep_wall(0, 0)
             keep_wall(1, 0)
             for copy in over_xy:
@@ -388,10 +401,10 @@
             for n in (1, 3, 5, 7):
                 third[n].wait_recv()
             dots(1, 4, 8)
-        if k == 15:
-            dots(2, 0, 4)
-    second[15].wait_recv()
-    third.append(start_stage(2, 15))
+    for k in range(16 - 3, 16):
+        second[k].wait_recv()
+        third.append(start_stage(2, k))
+    dots(2, 0, 4)
     dots(3, 0, 4)
     for s in (2, 3):
         for n in range(8, 16):
@@ -459,6 +472,7 @@
             pltpu.VMEM((2, 8, 256, 1024), BF),
             pltpu.VMEM((16, 8, 128), F32),
             pltpu.VMEM((8, 8, 128), F32),
+            pltpu.VMEM((36, 8, 128), F32),
             pltpu.SemaphoreType.DMA((22,)),
             pltpu.SemaphoreType.DMA((95,)),
             pltpu.SemaphoreType.DMA((95,)),
@@ -525,11 +539,12 @@
     for n, key in enumerate(order):
         one[key].wait_recv()
         two[key] = gather(1, *key)
-        if n >= 1:
-            two[order[n - 1]].wait_recv()
-            three[order[n - 1]] = gather(2, *order[n - 1])
-    two[order[7]].wait_recv()
-    three[order[7]] = gather(2, *order[7])
+        if n >= 3:
+            two[order[n - 3]].wait_recv()
+            three[order[n - 3]] = gather(2, *order[n - 3])
+    for key in order[8 - 3 :]:
+        two[key].wait_recv()
+        three[key] = gather(2, *key)
 
     def rows_of(r, cols):
         parts = [g[kind, r, :, :, cols].reshape(256, 256) for kind in range(2)]
@@ -612,10 +627,11 @@
 
     for n, key in enumerate(order):
         second(key)
-        if n >= 1:
-            third(order[n - 1])
+        if n >= 3:
+            third(order[n - 3])
         output_grad(n)
-    third(order[7])
+    for key in order[8 - 3 :]:
+        third(key)
     back = {}
     for rg in range(4):
         for kind in range(2):

time: 273 us -> 263 us (0.963)
  Pallas kernels: 272 us -> 262 us
    pallas_call x1, Pallas kernels: 112 us -> 108 us  [project(): pl.pallas_call(functools.partial(project_kernel, count), out_shape=(shape...]
    pallas_call x1, Pallas kernels: 79.9 us -> 76.1 us  [output_side(): pl.pallas_call(output_kernel, out_shape=(shape((2, 8, 32, 256), BF), shap...]
where the time goes in v6:
time: 263 us
  Pallas kernels  262 us (100%)
    pallas_call x1, Pallas kernels, project(): pl.pallas_call(functools.partial(project_kernel, count), out_shape=(shape...  108 us
    pallas_call x1, Pallas kernels, tail(): pl.pallas_call(functools.partial(tail_kernel, factor, count), out_shape=(...  76.4 us
    pallas_call x1, Pallas kernels, output_side(): pl.pallas_call(output_kernel, out_shape=(shape((2, 8, 32, 256), BF), shap...  76.1 us

profile of v6, /device:TPU:1, one launch (start us, length us, event | category | flops | bytes accessed | tf_op | source)
XLA Modules:
  0.0 263.2 jit_solution(12848445766246278103)
XLA Ops:
  0.6 107.6 %project.1 = (bf16[512,256]{1,0:T(8,128)(2,1)}, bf16[512,256]{1,0:T(8,128)(2,1)}, bf16[512,128]{1,0:T(8,128)(2,1)}, bf16[512,128]{1,0:T(8,128)(2,1)}, bf16[512,8...) custom-call(bf16[512,8192]{1,0:T(8,128)(2,1)} %bitcast.2, f32[1,8192]{1,0:T(1,128)} %bitcast.3, ...), custom_call_target="tpu_custom_call" | custom-call | tf_op jit(solution)/shard_map/project/pallas_call | solution.py:451
  108.3 76.1 %output_side.1 = (bf16[2,8,32,256]{3,2,1,0:T(8,128)(2,1)}, bf16[2,4,2,256,512]{4,3,2,1,0:T(8,128)(2,1)}, f32[4,256,256]{2,1,0:T(8,128)}) custom-call(bf16[512,256]{1,0:T(8,128)(2,1)} %get-tuple-element.17.q, bf16[512,256]{1,0:T(8,128)(2,1)} %get-tuple-element.18.t, bf16[512,128]{1,0:T(8,128)(2,1)} %get-tuple-element.19.k, ...), custom_call_target="tpu_custom_call" | custom-call | tf_op jit(solution)/shard_map/output_side/pallas_call | solution.py:655
  184.4 76.4 %tail.1 = (bf16[1024,256]{1,0:T(8,128)(2,1)}, bf16[256,1024]{1,0:T(8,128)(2,1)}, f32[16,128]{1,0:T(8,128)}) custom-call(bf16[512,8192]{1,0:T(8,128)(2,1)} %get-tuple-element.16.normed_hbm, bf16[2,8,32,256]{3,2,1,0:T(8,128)(2,1)} %get-tuple-element.22.cot_heads, bf16[512,128]{1,0:T(8,128)(2,1)} %get-tuple-element.19.k, bf16[512,128]{1,0:T(8,128)(2,1)} %get-tuple-element.20.v, ...), custom_call_target="tpu_custom_call" | custom-call | tf_op jit(solution)/shard_map/tail/pallas_call | solution.py:905
  260.8 2.2 finish.1

commit v7 on v6

--- a/solution.py
+++ b/solution.py
@@ -406,6 +406,10 @@
         third.append(start_stage(2, k))
     dots(2, 0, 4)
     dots(3, 0, 4)
+    for kind in range(2):
+        for piece in range(4):
+            out_copies[2, kind, piece].wait_recv()
+        keep_wall(kind, 4)
     for s in (2, 3):
         for n in range(8, 16):
             if SUPER[n] == s:
@@ -421,10 +425,6 @@
     first_core = core == 0
     k_out[...] = jnp.where(first_core, own, other).astype(BF)
     v_out[...] = jnp.where(first_core, other, own).astype(BF)
-    for kind in range(2):
-        for piece in range(4):
-            out_copies[2, kind, piece].wait_recv()
-        keep_wall(kind, 4)
     for copy in over_zc:
         copy.wait_recv()
     total = g2[0]
@@ -630,6 +630,8 @@
         if n >= 3:
             third(order[n - 3])
         output_grad(n)
+    gp_copy = pltpu.make_async_copy(gp, gp_out, load.at[2])
+    gp_copy.start()
     for key in order[8 - 3 :]:
         third(key)
     back = {}
@@ -641,8 +643,6 @@
             if r:
                 back[r] = start(r + 58, cs.at[:, r, 0], cot.at[:, place], same_core_masks(r))
     cot[:, place] = cs[:, 0, 0]
-    gp_copy = pltpu.make_async_copy(gp, gp_out, load.at[2])
-    gp_copy.start()
     for r in range(1, 8):
         back[r].wait_recv()
     for copy in copies:

time: 263 us -> 262 us (level)
  no operation moved by 1% of the time
where the time goes in v7:
time: 262 us; the launch traced here: 261 us
  Pallas kernels  261 us (100%)
    pallas_call x1, Pallas kernels, project(): pl.pallas_call(functools.partial(project_kernel, count), out_shape=(shape...  106 us
    pallas_call x1, Pallas kernels, tail(): pl.pallas_call(functools.partial(tail_kernel, factor, count), out_shape=(...  76.5 us
    pallas_call x1, Pallas kernels, output_side(): pl.pallas_call(output_kernel, out_shape=(shape((2, 8, 32, 256), BF), shap...  76.1 us

profile of v7, /device:TPU:1, one launch (start us, length us, event | category | flops | bytes accessed | tf_op | source)
XLA Modules:
  0.0 261.5 jit_solution(17986385348027062358)
XLA Ops:
  0.6 105.8 %project.1 = (bf16[512,256]{1,0:T(8,128)(2,1)}, bf16[512,256]{1,0:T(8,128)(2,1)}, bf16[512,128]{1,0:T(8,128)(2,1)}, bf16[512,128]{1,0:T(8,128)(2,1)}, bf16[512,8...) custom-call(bf16[512,8192]{1,0:T(8,128)(2,1)} %bitcast.2, f32[1,8192]{1,0:T(1,128)} %bitcast.3, ...), custom_call_target="tpu_custom_call" | custom-call | tf_op jit(solution)/shard_map/project/pallas_call | solution.py:451
  106.5 76.1 %output_side.1 = (bf16[2,8,32,256]{3,2,1,0:T(8,128)(2,1)}, bf16[2,4,2,256,512]{4,3,2,1,0:T(8,128)(2,1)}, f32[4,256,256]{2,1,0:T(8,128)}) custom-call(bf16[512,256]{1,0:T(8,128)(2,1)} %get-tuple-element.17.q, bf16[512,256]{1,0:T(8,128)(2,1)} %get-tuple-element.18.t, bf16[512,128]{1,0:T(8,128)(2,1)} %get-tuple-element.19.k, ...), custom_call_target="tpu_custom_call" | custom-call | tf_op jit(solution)/shard_map/output_side/pallas_call | solution.py:655
  182.6 76.5 %tail.1 = (bf16[1024,256]{1,0:T(8,128)(2,1)}, bf16[256,1024]{1,0:T(8,128)(2,1)}, f32[16,128]{1,0:T(8,128)}) custom-call(bf16[512,8192]{1,0:T(8,128)(2,1)} %get-tuple-element.16.normed_hbm, bf16[2,8,32,256]{3,2,1,0:T(8,128)(2,1)} %get-tuple-element.22.cot_heads, bf16[512,128]{1,0:T(8,128)(2,1)} %get-tuple-element.19.k, bf16[512,128]{1,0:T(8,128)(2,1)} %get-tuple-element.20.v, ...), custom_call_target="tpu_custom_call" | custom-call | tf_op jit(solution)/shard_map/tail/pallas_call | solution.py:905
  259.1 2.2 finish.1
